TPU v7x, 128 devices: a whole 4x4x4 slice. The times are simulated.
128 devices in a mesh: modes: 4 (over z_lo, core), rows: 32 (over x, z_hi, y).
Axes of the slice: x: 4, y: 4, z: 4 (z_hi: 2, z_lo: 2; z = z_hi * 2 + z_lo), core: 2. Of those that a mesh axis runs over, the one named last changes fastest.
Arguments:
- screens: float32 [2, 2048, 2048], P(None, 'rows'), may hold values from -6 to 6
- weights: float32 [8], P('modes'), may hold values from 0.05 to 0.5
Outputs:
- irradiance: float32 [2048, 2048], P('rows', 'modes')
All inputs are finite; a program needn't handle non-finite values.
Results may differ from a plain program's by a relative error of at most 0.0001.
Values sent between devices are 32-bit elements; how exact they have to be, the bound alone decides.
No kernel may reach another device: no remote copies, remote signals or barrier semaphores. Data moves between devices by JAX's collectives and lax.ppermute only.
A program may use at most 128 MiB of HBM per device.

v0:
```python
import math

import jax
import jax.numpy as jnp
import numpy as np
from jax import lax
from jax.experimental import pallas as pl
from jax.experimental.pallas import tpu as pltpu
from jax.sharding import PartitionSpec as P

N = 2048
RADIX = 8
BLOCK = N // RADIX
LANES = 128
GROUP = 16
MSG = 20
BOTH = ("rows", "modes")
AMPLITUDE = math.sqrt(8.0 / math.sqrt(math.pi / 2.0))
HALF = math.sqrt(0.5)


def block_tables():
    freq = np.arange(N)
    signed = np.where(freq >= N // 2, freq - N, freq)
    transfer = np.exp(-2j * np.pi * ((signed * signed) % (8 * N)) / (8 * N))
    offset = np.arange(384)[:, None] - 128 - np.arange(LANES)[None, :]
    bands = np.zeros((RADIX, 2, 384, LANES), np.float64)
    for j in range(RADIX):
        shifted = np.zeros(N, np.complex128)
        shifted[j::RADIX] = transfer[j::RADIX]
        impulse = np.fft.ifft(shifted)
        band = impulse[offset % N]
        bands[j, 0] = band.real
        bands[j, 1] = band.imag
    high = bands.astype(np.float32).astype(jnp.bfloat16)
    low = (bands - high.astype(np.float64)).astype(np.float32).astype(jnp.bfloat16)
    return high, low


def profile_table():
    coord = (np.arange(N) - (N / 2 - 0.5)) / (N / 8)
    scaled = coord * math.sqrt(2.0)
    polys = [np.ones_like(coord), 2.0 * scaled]
    for level in range(1, 3):
        polys.append(2.0 * scaled * polys[level] - 2.0 * level * polys[level - 1])
    rows = []
    for level in range(4):
        norm = math.sqrt(2.0**level * math.factorial(level))
        rows.append(polys[level] * np.exp(-coord * coord) * AMPLITUDE / norm)
    return np.stack(rows).astype(np.float32).reshape(4, 1, N)


def butterfly(x):
    def add(u, v):
        return (u[0] + v[0], u[1] + v[1])

    def sub(u, v):
        return (u[0] - v[0], u[1] - v[1])

    def down(u):
        return (u[1], -u[0])

    a = [add(x[q], x[q + 4]) for q in range(4)]
    b = [sub(x[q], x[q + 4]) for q in range(4)]
    c0, c1 = add(a[0], a[2]), sub(a[0], a[2])
    d0, d1 = add(a[1], a[3]), down(sub(a[1], a[3]))
    e1 = ((b[1][0] + b[1][1]) * HALF, (b[1][1] - b[1][0]) * HALF)
    e3 = ((b[3][1] - b[3][0]) * HALF, (b[3][0] + b[3][1]) * -HALF)
    e2 = down(b[2])
    f0, f1 = add(b[0], e2), sub(b[0], e2)
    g0, g1 = add(e1, e3), down(sub(e1, e3))
    return [
        add(c0, d0),
        add(f0, g0),
        add(c1, d1),
        add(f1, g1),
        sub(c0, d0),
        sub(f0, g0),
        sub(c1, d1),
        sub(f1, g1),
    ]


def unbutterfly(y):
    return [(z[1], z[0]) for z in butterfly([(v[1], v[0]) for v in y])]


def sincos(x):
    turns = jnp.floor(x * (2.0 / math.pi) + 0.5)
    r = x - turns * 1.5703125
    r = r - turns * 4.837512969970703125e-4
    r = r - turns * 7.54978995489188216e-8
    quadrant = turns.astype(jnp.int32)
    z = r * r
    s = ((-1.9515295891e-4 * z + 8.3321608736e-3) * z - 1.6666654611e-1) * z * r + r
    c = ((2.443315711809948e-5 * z - 1.388731625493765e-3) * z + 4.166664568298827e-2) * z * z
    c = c - 0.5 * z + 1.0
    odd = (quadrant & 1) == 1
    sine = jnp.where(odd, c, s)
    cosine = jnp.where(odd, s, c)
    sine = jnp.where((quadrant & 2) == 2, -sine, sine)
    cosine = jnp.where(((quadrant + 1) & 2) == 2, -cosine, cosine)
    return sine, cosine


def split(value):
    high = value.astype(jnp.bfloat16)
    low = (value - high.astype(jnp.float32)).astype(jnp.bfloat16)
    return high, low


def lane_groups(shape):
    return lax.broadcasted_iota(jnp.int32, shape, 1) // GROUP


def swap_groups(rows):
    rows = list(rows)
    groups = lane_groups(rows[0].shape)
    for step in (1, 2, 4):
        keep = (groups & step) == 0
        for k in range(8):
            if k & step == 0:
                low, high = rows[k], rows[k + step]
                rows[k] = jnp.where(keep, low, pltpu.roll(high, step * GROUP, 1))
                rows[k + step] = jnp.where(
                    keep, pltpu.roll(low, LANES - step * GROUP, 1), high
                )
    return rows


def matrix(table_ref, j, part):
    return jnp.concatenate(
        [table_ref[j, part, 128:384, :], table_ref[j, part, 0:256, :]], axis=1
    )


def dot(left, right):
    return jnp.dot(left, right, preferred_element_type=jnp.float32)


def blocks_on_lanes(half, zh_ref, zl_ref, hi_ref, lo_ref, y_ref):
    def body(j, carry):
        t = lax.rem(RADIX - j, RADIX)
        zh, zl = zh_ref[j], zl_ref[j]
        wrh, wih = matrix(hi_ref, t, 0), matrix(hi_ref, t, 1)
        wrl, wil = matrix(lo_ref, t, 0), matrix(lo_ref, t, 1)
        pr = dot(zh, wrh) + dot(zl, wrh) + dot(zh, wrl)
        pi = dot(zh, wih) + dot(zl, wih) + dot(zh, wil)
        y_ref[j, 0] = pr[:half] - pi[half:]
        y_ref[j, 1] = pi[:half] + pr[half:]
        return carry

    lax.fori_loop(0, RADIX, body, 0)


def blocks_on_sublanes(zh_ref, zl_ref, hi_ref, lo_ref, y_ref):
    def body(j, carry):
        zh, zl = zh_ref[j], zl_ref[j]
        brh, bih = matrix(hi_ref, j, 0), matrix(hi_ref, j, 1)
        brl, bil = matrix(lo_ref, j, 0), matrix(lo_ref, j, 1)
        tr = dot(brh, zh) + dot(brh, zl) + dot(brl, zh)
        ti = dot(bih, zh) + dot(bih, zl) + dot(bil, zh)
        y_ref[j, 0] = tr[:, :LANES] - ti[:, LANES:]
        y_ref[j, 1] = tr[:, LANES:] + ti[:, :LANES]
        return carry

    lax.fori_loop(0, RADIX, body, 0)


def first_kernel(
    screens_ref, prof_ref, hi_ref, lo_ref, out_ref, cs_ref, e_ref, zh_ref, zl_ref, y_ref, t_ref
):
    m = lax.axis_index("modes")
    r = lax.axis_index("rows")
    rows = pl.ds(pl.multiple_of(m * 16, 16), 16)
    cell = lax.broadcasted_iota(jnp.int32, (16, LANES), 0) + (r * 64 + m * 16)
    coord = (cell.astype(jnp.float32) - (N / 2 - 0.5)) / (N / 8)
    envelope = jnp.exp(-coord * coord) * AMPLITUDE

    def screens(t, carry):
        lanes = pl.ds(pl.multiple_of(t * LANES, LANES), LANES)
        sine, cosine = sincos(screens_ref[0, rows, lanes])
        cs_ref[0, t] = cosine * envelope
        cs_ref[1, t] = sine * envelope
        sine, cosine = sincos(screens_ref[1, rows, lanes])
        e_ref[t, 0] = cosine
        e_ref[t, 1] = sine
        return carry

    lax.fori_loop(0, 16, screens, 0)

    def forward(i, carry):
        b, h = i // 2, i % 2
        lanes = pl.ds(pl.multiple_of(h * LANES, LANES), LANES)
        xs = []
        for q in range(RADIX):
            at = pl.ds(pl.multiple_of(q * BLOCK + h * LANES, LANES), LANES)
            weight = prof_ref[b, :, at]
            xs.append((cs_ref[0, q * 2 + h] * weight, cs_ref[1, q * 2 + h] * weight))
        for j, pair in enumerate(butterfly(xs)):
            for c in range(2):
                at = pl.ds(pl.multiple_of(c * 64 + b * 16, 16), 16)
                high, low = split(pair[c])
                zh_ref[j, at, lanes] = high
                zl_ref[j, at, lanes] = low
        return carry

    lax.fori_loop(0, 8, forward, 0)
    blocks_on_lanes(64, zh_ref, zl_ref, hi_ref, lo_ref, y_ref)

    def backward(i, carry):
        b, h = i // 2, i % 2
        lanes = pl.ds(pl.multiple_of(h * LANES, LANES), LANES)
        at = pl.ds(pl.multiple_of(b * 16, 16), 16)
        ys = [(y_ref[j, 0, at, lanes], y_ref[j, 1, at, lanes]) for j in range(RADIX)]
        for q, pair in enumerate(unbutterfly(ys)):
            t_ref[q * 2 + h, b] = pair[0]
            t_ref[q * 2 + h, 4 + b] = pair[1]
        return carry

    lax.fori_loop(0, 8, backward, 0)
    parity = m % 2

    def pack(t, carry):
        base = t * (8 * MSG)
        fields = swap_groups([t_ref[t, k] for k in range(8)])
        phases = swap_groups(
            [e_ref[t, k % 2, pl.ds(k // 2, 4, stride=4), :] for k in range(8)]
        )
        for k in range(8):
            out_ref[pl.ds(base + k * MSG + parity * 4, 16), :] = fields[k]
            out_ref[pl.ds(base + k * MSG + (1 - parity) * 16, 4), :] = phases[k]
        return carry

    lax.fori_loop(0, 16, pack, 0)


def second_kernel(in_ref, hi_ref, lo_ref, out_ref, e_ref, zh_ref, zl_ref, y_ref):
    groups = lane_groups((8, LANES))

    def phases(p, carry):
        packed = in_ref[pl.ds(pl.multiple_of(p * 40 + 16, 8), 8), :]
        level = [packed]
        for step in (4, 2, 1):
            keep = (groups & step) == 0
            following = []
            for value in level:
                moved = pltpu.roll(value, step * GROUP, 1)
                following.append(jnp.where(keep, value, moved))
                following.append(jnp.where(keep, moved, value))
            level = following
        for k in range(8):
            e_ref[k % 2, pl.ds(p * 32 + k // 2, 8, stride=4), :] = level[k]
        return carry

    lax.fori_loop(0, 64, phases, 0)
    left = lax.broadcasted_iota(jnp.int32, (16, LANES), 1) < 64
    line = lax.broadcasted_iota(jnp.int32, (16, LANES), 0)

    def store(at, pairs):
        for j, pair in enumerate(pairs):
            for c in range(2):
                high, low = split(pair[c])
                zh_ref[j, at, c * LANES : (c + 1) * LANES] = high
                zl_ref[j, at, c * LANES : (c + 1) * LANES] = low

    def load(at):
        return unbutterfly([(y_ref[j, 0, at, :], y_ref[j, 1, at, :]) for j in range(RADIX)])

    def forward(p, carry):
        for u in range(2):
            xs = []
            for q in range(RADIX):
                row = pl.multiple_of(p * 40 + (q * 320 + u * 24), 8)
                value = in_ref[pl.ds(row, 16), :]
                moved = pltpu.roll(value, 64, 1)
                cell = (line + (q * BLOCK + u * 16 + p * 32)).astype(jnp.float32)
                factor = jnp.where(left, 1.0, (cell - (N / 2 - 0.5)) * (2.0 / (N / 8)))
                xs.append((jnp.where(left, value, moved) * factor, jnp.where(left, moved, value) * factor))
            store(pl.ds(pl.multiple_of(p * 32 + u * 16, 16), 16), butterfly(xs))
        return carry

    lax.fori_loop(0, 8, forward, 0)
    blocks_on_sublanes(zh_ref, zl_ref, hi_ref, lo_ref, y_ref)

    def middle(s, carry):
        at = pl.ds(pl.multiple_of(s * 16, 16), 16)
        xs = []
        for q, (re, im) in enumerate(load(at)):
            here = pl.ds(pl.multiple_of(s * 16 + q * BLOCK, 16), 16)
            cosine, sine = e_ref[0, here, :], e_ref[1, here, :]
            xs.append((re * cosine - im * sine, re * sine + im * cosine))
        store(at, butterfly(xs))
        return carry

    lax.fori_loop(0, 16, middle, 0)
    blocks_on_sublanes(zh_ref, zl_ref, hi_ref, lo_ref, y_ref)

    def backward(s, carry):
        at = pl.ds(pl.multiple_of(s * 16, 16), 16)
        for q, (re, im) in enumerate(load(at)):
            row = pl.multiple_of(s * 32 + q * 512, 32)
            out_ref[pl.ds(row, 16), :] = re
            out_ref[pl.ds(row + 16, 16), :] = im
        return carry

    lax.fori_loop(0, 16, backward, 0)


def third_kernel(
    in_ref, weight_ref, hi_ref, lo_ref, out0, out1, out2, out3, t_ref, zh_ref, zl_ref, y_ref, i_ref
):
    m = lax.axis_index("modes")

    def unpack(t, carry):
        for c in range(2):
            values = [
                in_ref[pl.ds(pl.multiple_of(t * 256 + (s * 32 + c * 16), 16), 16), :]
                for s in range(8)
            ]
            for k, value in enumerate(swap_groups(values)):
                t_ref[t, c, k] = value
        return carry

    lax.fori_loop(0, 16, unpack, 0)

    def forward(i, carry):
        mode, h = i // 2, i % 2
        lanes = pl.ds(pl.multiple_of(h * LANES, LANES), LANES)
        xs = [(t_ref[q * 2 + h, 0, mode], t_ref[q * 2 + h, 1, mode]) for q in range(RADIX)]
        for j, pair in enumerate(butterfly(xs)):
            for c in range(2):
                at = pl.ds(pl.multiple_of(c * 128 + mode * 16, 16), 16)
                high, low = split(pair[c])
                zh_ref[j, at, lanes] = high
                zl_ref[j, at, lanes] = low
        return carry

    lax.fori_loop(0, 16, forward, 0)
    blocks_on_lanes(128, zh_ref, zl_ref, hi_ref, lo_ref, y_ref)
    for t in range(16):
        i_ref[t] = jnp.zeros((16, LANES), jnp.float32)

    def backward(i, carry):
        mode, h = i // 2, i % 2
        lanes = pl.ds(pl.multiple_of(h * LANES, LANES), LANES)
        at = pl.ds(pl.multiple_of(mode * 16, 16), 16)
        weight = weight_ref[jnp.bitwise_xor(m, mode // 2), mode % 2]
        ys = [(y_ref[j, 0, at, lanes], y_ref[j, 1, at, lanes]) for j in range(RADIX)]
        for q, (re, im) in enumerate(unbutterfly(ys)):
            i_ref[q * 2 + h] += weight * (re * re + im * im)
        return carry

    lax.fori_loop(0, 16, backward, 0)
    for k, out_ref in enumerate((out0, out1, out2, out3)):
        owner = jnp.bitwise_xor(m, k)
        for t in range(4):
            out_ref[:, t * LANES : (t + 1) * LANES] = i_ref[owner * 4 + t]


def last_kernel(in0, in1, in2, in3, out_ref):
    m = lax.axis_index("modes")
    for k, in_ref in enumerate((in0, in1, in2, in3)):
        row = pl.multiple_of(jnp.bitwise_xor(m, k) * 16, 16)
        out_ref[pl.ds(row, 16), :] = in_ref[...]


def f32(*shape):
    return jax.ShapeDtypeStruct(shape, jnp.float32)


def exchange(value):
    return lax.all_to_all(value, BOTH, split_axis=0, concat_axis=0, tiled=True)


def partner(value, k):
    return lax.ppermute(value, "modes", [(i, i ^ k) for i in range(4)])


def shards(screens, weights):
    high, low = (jnp.asarray(table) for table in block_tables())
    profiles = jnp.asarray(profile_table())
    vmem = pl.BlockSpec(memory_space=pltpu.VMEM)
    smem = pl.BlockSpec(memory_space=pltpu.SMEM)
    z_scratch = [pltpu.VMEM((RADIX, 256, 256), jnp.bfloat16)] * 2

    mine = weights.reshape(1, 2)
    everyone = jnp.concatenate([mine] + [partner(mine, k) for k in (1, 2, 3)])

    sent = pl.pallas_call(
        first_kernel,
        out_shape=f32(128 * MSG, LANES),
        in_specs=[vmem] * 4,
        out_specs=vmem,
        scratch_shapes=[
            pltpu.VMEM((2, 16, 16, LANES), jnp.float32),
            pltpu.VMEM((16, 2, 16, LANES), jnp.float32),
            pltpu.VMEM((RADIX, 128, 256), jnp.bfloat16),
            pltpu.VMEM((RADIX, 128, 256), jnp.bfloat16),
            pltpu.VMEM((RADIX, 2, 64, 256), jnp.float32),
            pltpu.VMEM((16, 8, 16, LANES), jnp.float32),
        ],
        name="first",
    )(screens, profiles, high, low)
    got = exchange(sent.reshape(128 * MSG, 1, LANES)).reshape(128 * MSG, LANES)

    sent = pl.pallas_call(
        second_kernel,
        out_shape=f32(128 * 32, LANES),
        in_specs=[vmem] * 3,
        out_specs=vmem,
        scratch_shapes=[pltpu.VMEM((2, N, LANES), jnp.float32)]
        + z_scratch
        + [pltpu.VMEM((RADIX, 2, 256, LANES), jnp.float32)],
        name="second",
    )(got, high, low)
    got = exchange(sent.reshape(128, 32, LANES)).reshape(128 * 32, LANES)

    pieces = pl.pallas_call(
        third_kernel,
        out_shape=[f32(16, 512)] * 4,
        in_specs=[vmem, smem, vmem, vmem],
        out_specs=[vmem] * 4,
        scratch_shapes=[pltpu.VMEM((16, 2, 8, 16, LANES), jnp.float32)]
        + z_scratch
        + [
            pltpu.VMEM((RADIX, 2, 128, 256), jnp.float32),
            pltpu.VMEM((16, 16, LANES), jnp.float32),
        ],
        name="third",
    )(got, everyone, high, low)
    pieces = [pieces[0]] + [partner(pieces[k], k) for k in (1, 2, 3)]

    return pl.pallas_call(
        last_kernel,
        out_shape=f32(64, 512),
        in_specs=[vmem] * 4,
        out_specs=vmem,
        name="last",
    )(*pieces)


def solution(mesh):
    return jax.shard_map(
        shards,
        mesh=mesh,
        in_specs=(P(None, "rows", None), P("modes")),
        out_specs=P("rows", "modes"),
        check_vma=False,
    )
```

profile of v0, /device:TPU:1, one launch (start us, length us, event | category | flops | bytes accessed | tf_op | source)
XLA Modules:
  0.0 124.8 jit_solution(13327164417693040122)
XLA Ops:
  0.0 10.5 %first.1 = f32[2560,128]{1,0:T(8,128)} custom-call(f32[2,64,2048]{2,1,0:T(8,128)} %screens_ref.1, f32[4,1,2048]{2,1,0:T(1,128)} %constant.8.clone.prof_ref, bf16[8,2,384,128]{3,2,1,0:T(8,128)(2,1)} %constant.6.clone.hi_ref, bf16[8,2,384,128]{3,2,1,0:T(8,128)(2,1)} %constant.7.clone.lo_ref), custom_call_target="tpu_custom_call" | custom-call | tf_op jit(solution)/shard_map/first/pallas_call | solution.py:390
  10.5 33.7 %all_to_all.10 = f32[2560,1,128]{2,1,0:T(1,128)} all-to-all(f32[2560,1,128]{2,1,0:T(1,128)} %bitcast.9), channel_id=1, replica_groups=mesh['modes'=4,'rows'=32] {'rows','modes'}, dimensions={0} | all-to-all | bytes 2621440 | tf_op jit(solution)/shard_map/all_to_all | solution.py:373
  44.1 25.9 %second.1 = f32[4096,128]{1,0:T(8,128)} custom-call(f32[2560,128]{1,0:T(8,128)} %bitcast.10, bf16[8,2,384,128]{3,2,1,0:T(8,128)(2,1)} %constant.6.clone.hi_ref, bf16[8,2,384,128]{3,2,1,0:T(8,128)(2,1)} %constant.7.clone.lo_ref), custom_call_target="tpu_custom_call" | custom-call | tf_op jit(solution)/shard_map/second/pallas_call | solution.py:407
  70.1 0.0 copy-start.4
  70.1 4.1 %all-to-all-start.1 = ((f32[128,32,128]{2,1,0:T(8,128)}), f32[128,32,128]{2,1,0:T(8,128)S(1)}, u32[]{:S(2)}, u32[]{:S(2)}) async-start(f32[128,32,128]{2,1,0:T(8,128)} %bitcast.8), calls=%async_computation.1 | async-start | bytes 4194304 | tf_op jit(solution)/shard_map/all_to_all | solution.py:373
  74.2 0.0 copy-done.4
  74.2 2.0 %collective-permute-start.2 = (f32[1,2]{1,0:T(1,128)S(1)}, f32[1,2]{1,0:T(1,128)S(1)}, u32[]{:S(2)}, u32[]{:S(2)}) collective-permute-start(f32[1,2]{1,0:T(1,128)S(1)} %bitcast.11), channel_id=1, source_target_pairs={{0,96},{32,64},{64,32},{96,0},{1,97},{33,65},{65,33},{97,1},{2,98}... | collective-permute-start | bytes 32 | tf_op jit(solution)/shard_map/ppermute | solution.py:377
  76.2 0.7 collective-permute-start.1
  76.8 0.0 collective-permute-start
  76.8 2.2 %collective-permute-done.2 = f32[1,2]{1,0:T(1,128)S(1)} collective-permute-done((f32[1,2]{1,0:T(1,128)S(1)}, f32[1,2]{1,0:T(1,128)S(1)}, u32[]{:S(2)}, u32[]{:S(2)}) %collective-permute-start.2) | collective-permute-done | bytes 40 | tf_op jit(solution)/shard_map/ppermute | solution.py:377
  79.1 0.0 collective-permute-done.1
  79.1 0.0 collective-permute-done
  79.1 0.6 pad_maximum_fusion.weight_ref
  79.7 24.4 %all-to-all-done.1 = f32[128,32,128]{2,1,0:T(8,128)S(1)} async-done(((f32[128,32,128]{2,1,0:T(8,128)}), f32[128,32,128]{2,1,0:T(8,128)S(1)}, u32[]{:S(2)}, u32[]{:S(2)}) %all-to-all-start.1) | async-done | bytes 2097184 | tf_op jit(solution)/shard_map/all_to_all | solution.py:373
  104.1 0.0 copy-start
  104.1 1.3 %copy-done = f32[128,32,128]{2,1,0:T(8,128)} copy-done((f32[128,32,128]{2,1,0:T(8,128)}, f32[128,32,128]{2,1,0:T(8,128)S(1)}, u32[]{:S(2)}) %copy-start) | copy-done | bytes 2097176
  105.4 11.7 %third.1 = (f32[16,512]{1,0:T(8,128)}, f32[16,512]{1,0:T(8,128)}, f32[16,512]{1,0:T(8,128)}, f32[16,512]{1,0:T(8,128)}) custom-call(f32[4096,128]{1,0:T(8,128)} %bitcast.7, f32[4,2]{1,0:T(4,128)} %pad_maximum_fusion.weight_ref, bf16[8,2,384,128]{3,2,1,0:T(8,128)(2,1)} %constant.6.clone.hi_ref, bf16[8,2,384,128]{3,2,1,0:T(8,128)(2,1)} %constant.7.clone.lo_ref), custom_call_target="tpu_custom_call" | custom-call | tf_op jit(solution)/shard_map/third/pallas_call | solution.py:419
  117.2 1.2 collective-permute-start.3
  118.4 0.5 collective-permute-start.4
  118.9 1.2 collective-permute-start.5
  120.1 0.0 collective-permute-done.3.in1
  120.1 0.0 copy-start.1
  120.1 1.3 %collective-permute-done.4.in2 = f32[16,512]{1,0:T(8,128)S(1)} collective-permute-done((f32[16,512]{1,0:T(8,128)}, f32[16,512]{1,0:T(8,128)S(1)}, u32[]{:S(2)}, u32[]{:S(2)}) %collective-permute-start.4) | collective-permute-done | bytes 32800 | tf_op jit(solution)/shard_map/ppermute | solution.py:377
  121.4 0.0 copy-start.2
  121.4 1.3 %collective-permute-done.5.in3 = f32[16,512]{1,0:T(8,128)S(1)} collective-permute-done((f32[16,512]{1,0:T(8,128)}, f32[16,512]{1,0:T(8,128)S(1)}, u32[]{:S(2)}, u32[]{:S(2)}) %collective-permute-start.5) | collective-permute-done | bytes 32800 | tf_op jit(solution)/shard_map/ppermute | solution.py:377
  122.7 0.0 copy-start.3
  122.7 0.0 copy-done.1
  122.7 0.0 copy-done.2
  122.7 0.6 copy-done.3
  123.3 1.5 %last.1 = f32[64,512]{1,0:T(8,128)} custom-call(f32[16,512]{1,0:T(8,128)} %get-tuple-element.9.in0, f32[16,512]{1,0:T(8,128)} %copy-done.1, f32[16,512]{1,0:T(8,128)} %copy-done.2, f32[16,512]{1,0:T(8,128)} %copy-done.3), custom_call_target="tpu_custom_call" | custom-call | tf_op jit(solution)/shard_map/last/pallas_call | solution.py:434
Async XLA Ops:
  70.1 4.1 %copy-start.4 = (f32[2]{0:T(128)S(1)}, f32[2]{0:T(128)}, u32[]{:S(2)}) copy-start(f32[2]{0:T(128)} %param.6) | copy-start | bytes 28
  70.1 34.0 %all-to-all-start.1 = ((f32[128,32,128]{2,1,0:T(8,128)}), f32[128,32,128]{2,1,0:T(8,128)S(1)}, u32[]{:S(2)}, u32[]{:S(2)}) async-start(f32[128,32,128]{2,1,0:T(8,128)} %bitcast.8), calls=%async_computation.1 | async-start | bytes 4194304 | tf_op jit(solution)/shard_map/all_to_all | solution.py:373
  74.2 4.9 %collective-permute-start.2 = (f32[1,2]{1,0:T(1,128)S(1)}, f32[1,2]{1,0:T(1,128)S(1)}, u32[]{:S(2)}, u32[]{:S(2)}) collective-permute-start(f32[1,2]{1,0:T(1,128)S(1)} %bitcast.11), channel_id=1, source_target_pairs={{0,96},{32,64},{64,32},{96,0},{1,97},{33,65},{65,33},{97,1},{2,98}... | collective-permute-start | bytes 32 | tf_op jit(solution)/shard_map/ppermute | solution.py:377
  76.2 2.9 %collective-permute-start.1 = (f32[1,2]{1,0:T(1,128)S(1)}, f32[1,2]{1,0:T(1,128)S(1)}, u32[]{:S(2)}, u32[]{:S(2)}) collective-permute-start(f32[1,2]{1,0:T(1,128)S(1)} %bitcast.12), channel_id=1, source_target_pairs={{0,64},{32,96},{64,0},{96,32},{1,65},{33,97},{65,1},{97,33},{2,66}... | collective-permute-start | bytes 32 | tf_op jit(solution)/shard_map/ppermute | solution.py:377
  76.8 2.2 %collective-permute-start = (f32[1,2]{1,0:T(1,128)S(1)}, f32[1,2]{1,0:T(1,128)S(1)}, u32[]{:S(2)}, u32[]{:S(2)}) collective-permute-start(f32[1,2]{1,0:T(1,128)S(1)} %bitcast.13), channel_id=1, source_target_pairs={{0,32},{32,0},{64,96},{96,64},{1,33},{33,1},{65,97},{97,65},{2,34}... | collective-permute-start | bytes 32 | tf_op jit(solution)/shard_map/ppermute | solution.py:377
  104.1 1.3 %copy-start = (f32[128,32,128]{2,1,0:T(8,128)}, f32[128,32,128]{2,1,0:T(8,128)S(1)}, u32[]{:S(2)}) copy-start(f32[128,32,128]{2,1,0:T(8,128)S(1)} %all-to-all-done.1) | copy-start | bytes 6291460
  117.2 2.9 %collective-permute-start.3 = (f32[16,512]{1,0:T(8,128)}, f32[16,512]{1,0:T(8,128)S(1)}, u32[]{:S(2)}, u32[]{:S(2)}) collective-permute-start(f32[16,512]{1,0:T(8,128)} %get-tuple-element.10), channel_id=1, source_target_pairs={{0,32},{32,0},{64,96},{96,64},{1,33},{33,1},{65,97},{97,65},{2,34}... | collective-permute-start | bytes 98312 | tf_op jit(solution)/shard_map/ppermute | solution.py:377
  118.4 3.0 %collective-permute-start.4 = (f32[16,512]{1,0:T(8,128)}, f32[16,512]{1,0:T(8,128)S(1)}, u32[]{:S(2)}, u32[]{:S(2)}) collective-permute-start(f32[16,512]{1,0:T(8,128)} %get-tuple-element.11), channel_id=1, source_target_pairs={{0,64},{32,96},{64,0},{96,32},{1,65},{33,97},{65,1},{97,33},{2,66}... | collective-permute-start | bytes 98312 | tf_op jit(solution)/shard_map/ppermute | solution.py:377
  118.9 3.7 %collective-permute-start.5 = (f32[16,512]{1,0:T(8,128)}, f32[16,512]{1,0:T(8,128)S(1)}, u32[]{:S(2)}, u32[]{:S(2)}) collective-permute-start(f32[16,512]{1,0:T(8,128)} %get-tuple-element.12), channel_id=1, source_target_pairs={{0,96},{32,64},{64,32},{96,0},{1,97},{33,65},{65,33},{97,1},{2,98}... | collective-permute-start | bytes 98312 | tf_op jit(solution)/shard_map/ppermute | solution.py:377
  120.1 2.6 %copy-start.1 = (f32[16,512]{1,0:T(8,128)}, f32[16,512]{1,0:T(8,128)S(1)}, u32[]{:S(2)}) copy-start(f32[16,512]{1,0:T(8,128)S(1)} %collective-permute-done.3.in1) | copy-start | bytes 98308
  121.4 1.3 %copy-start.2 = (f32[16,512]{1,0:T(8,128)}, f32[16,512]{1,0:T(8,128)S(1)}, u32[]{:S(2)}) copy-start(f32[16,512]{1,0:T(8,128)S(1)} %collective-permute-done.4.in2) | copy-start | bytes 98308
  122.7 0.6 copy-start.3
where the time goes:
time: 125 us
  Pallas kernels  49.6 us (40%)
  blocking collectives  33.7 us (27%)
  waiting for transfers between devices  29.3 us (23%)
  starting transfers between devices  9.66 us (8%)
  local copies, waits for them, and re-layouts  1.93 us (2%)
    all_to_all x1, blocking collectives, exchange(): return lax.all_to_all(value, BOTH, split_axis=0, concat_axis=0, tiled=True)  33.7 us
    pallas_call x1, Pallas kernels, shards(): pl.pallas_call(second_kernel, out_shape=f32(128 * 32, LANES), in_specs=[v...  25.9 us
    all_to_all x1, waiting for transfers between devices, exchange(): return lax.all_to_all(value, BOTH, split_axis=0, concat_axis=0, tiled=True)  24.4 us
    pallas_call x1, Pallas kernels, shards(): pl.pallas_call(third_kernel, out_shape=[f32(16, 512)] * 4, in_specs=[vmem...  11.7 us
    pallas_call x1, Pallas kernels, shards(): pl.pallas_call(first_kernel, out_shape=f32(128 * MSG, LANES), in_specs=[v...  10.5 us
    ppermute x6, starting transfers between devices, partner(): return lax.ppermute(value, 'modes', [(i, i ^ k) for i in range(4)])  5.58 us
    ppermute x6, waiting for transfers between devices, partner(): return lax.ppermute(value, 'modes', [(i, i ^ k) for i in range(4)])  4.81 us
    all_to_all x1, starting transfers between devices, exchange(): return lax.all_to_all(value, BOTH, split_axis=0, concat_axis=0, tiled=True)  4.09 us
  transfers between devices with their start and end apart: 7, of which 4 were waited for; matrix products, arithmetic and copies ran while one was open for 0% of the time, Pallas kernels for 0%

commit v1 on v0

v1 whole, which is shorter than its diff:
```python
import math

import jax
import jax.numpy as jnp
import numpy as np
from jax import lax
from jax.experimental import pallas as pl
from jax.experimental.pallas import tpu as pltpu
from jax.sharding import PartitionSpec as P

N = 2048
RADIX = 8
BLOCK = N // RADIX
LANES = 128
GROUP = 16
MSG = 18
BOTH = ("rows", "modes")
AMPLITUDE = math.sqrt(8.0 / math.sqrt(math.pi / 2.0))
HALF = math.sqrt(0.5)


def params(mib):
    return pltpu.CompilerParams(vmem_limit_bytes=mib * 2**20)


def block_tables():
    freq = np.arange(N)
    signed = np.where(freq >= N // 2, freq - N, freq)
    transfer = np.exp(-2j * np.pi * ((signed * signed) % (8 * N)) / (8 * N))
    offset = np.arange(384)[:, None] - 128 - np.arange(LANES)[None, :]
    bands = np.zeros((RADIX, 2, 384, LANES), np.float64)
    for j in range(RADIX):
        shifted = np.zeros(N, np.complex128)
        shifted[j::RADIX] = transfer[j::RADIX]
        impulse = np.fft.ifft(shifted)
        band = impulse[offset % N]
        bands[j, 0] = band.real
        bands[j, 1] = band.imag
    high = bands.astype(np.float32).astype(jnp.bfloat16)
    low = (bands - high.astype(np.float64)).astype(np.float32).astype(jnp.bfloat16)
    return high, low


def profile_table():
    coord = (np.arange(N) - (N / 2 - 0.5)) / (N / 8)
    scaled = coord * math.sqrt(2.0)
    polys = [np.ones_like(coord), 2.0 * scaled]
    for level in range(1, 3):
        polys.append(2.0 * scaled * polys[level] - 2.0 * level * polys[level - 1])
    rows = []
    for level in range(4):
        norm = math.sqrt(2.0**level * math.factorial(level))
        rows.append(polys[level] * np.exp(-coord * coord) * AMPLITUDE / norm)
    return np.stack(rows).astype(np.float32).reshape(4, 1, N)


def butterfly(x):
    def add(u, v):
        return (u[0] + v[0], u[1] + v[1])

    def sub(u, v):
        return (u[0] - v[0], u[1] - v[1])

    def down(u):
        return (u[1], -u[0])

    a = [add(x[q], x[q + 4]) for q in range(4)]
    b = [sub(x[q], x[q + 4]) for q in range(4)]
    c0, c1 = add(a[0], a[2]), sub(a[0], a[2])
    d0, d1 = add(a[1], a[3]), down(sub(a[1], a[3]))
    e1 = ((b[1][0] + b[1][1]) * HALF, (b[1][1] - b[1][0]) * HALF)
    e3 = ((b[3][1] - b[3][0]) * HALF, (b[3][0] + b[3][1]) * -HALF)
    e2 = down(b[2])
    f0, f1 = add(b[0], e2), sub(b[0], e2)
    g0, g1 = add(e1, e3), down(sub(e1, e3))
    return [
        add(c0, d0),
        add(f0, g0),
        add(c1, d1),
        add(f1, g1),
        sub(c0, d0),
        sub(f0, g0),
        sub(c1, d1),
        sub(f1, g1),
    ]


def unbutterfly(y):
    return [(z[1], z[0]) for z in butterfly([(v[1], v[0]) for v in y])]


def sincos(x):
    turns = jnp.floor(x * (2.0 / math.pi) + 0.5)
    r = x - turns * 1.5703125
    r = r - turns * 4.837512969970703125e-4
    r = r - turns * 7.54978995489188216e-8
    quadrant = turns.astype(jnp.int32)
    z = r * r
    s = ((-1.9515295891e-4 * z + 8.3321608736e-3) * z - 1.6666654611e-1) * z * r + r
    c = ((2.443315711809948e-5 * z - 1.388731625493765e-3) * z + 4.166664568298827e-2) * z * z
    c = c - 0.5 * z + 1.0
    odd = (quadrant & 1) == 1
    sine = jnp.where(odd, c, s)
    cosine = jnp.where(odd, s, c)
    sine = jnp.where((quadrant & 2) == 2, -sine, sine)
    cosine = jnp.where(((quadrant + 1) & 2) == 2, -cosine, cosine)
    return sine, cosine


def split(value):
    high = value.astype(jnp.bfloat16)
    low = (value - high.astype(jnp.float32)).astype(jnp.bfloat16)
    return high, low


def lane_groups(shape):
    return lax.broadcasted_iota(jnp.int32, shape, 1) // GROUP


def swap_groups(rows):
    groups = lane_groups(rows[0].shape)
    rows = [rows[0]] + [pltpu.roll(rows[k], k * GROUP, 1) for k in range(1, 8)]
    for step in (1, 2, 4):
        moves = (groups & step) != 0
        rows = [jnp.where(moves, rows[(k + step) % 8], rows[k]) for k in range(8)]
    return [rows[0]] + [pltpu.roll(rows[8 - k], LANES - k * GROUP, 1) for k in range(1, 8)]


def matrix(table_ref, j, part):
    return jnp.concatenate(
        [table_ref[j, part, 128:384, :], table_ref[j, part, 0:256, :]], axis=1
    )


def dot(left, right):
    return jnp.dot(left, right, preferred_element_type=jnp.float32)


def blocks_on_lanes(half, zh_ref, zl_ref, hi_ref, lo_ref, y_ref, wait=None):
    def body(j, carry):
        t = lax.rem(RADIX - j, RADIX)
        if wait is not None:
            wait(t)
        zh = jnp.concatenate([zh_ref[j, 0], zh_ref[j, 1]], axis=1)
        zl = jnp.concatenate([zl_ref[j, 0], zl_ref[j, 1]], axis=1)
        wrh, wih = matrix(hi_ref, t, 0), matrix(hi_ref, t, 1)
        wrl, wil = matrix(lo_ref, t, 0), matrix(lo_ref, t, 1)
        both = jnp.concatenate([zh, zl], axis=0)
        pr, pi = dot(both, wrh), dot(both, wih)
        pr = pr[: 2 * half] + pr[2 * half :] + dot(zh, wrl)
        pi = pi[: 2 * half] + pi[2 * half :] + dot(zh, wil)
        re = pr[:half] - pi[half:]
        im = pi[:half] + pr[half:]
        for h in range(2):
            y_ref[j, 0, h] = re[:, h * LANES : (h + 1) * LANES]
            y_ref[j, 1, h] = im[:, h * LANES : (h + 1) * LANES]
        return carry

    lax.fori_loop(0, RADIX, body, 0)


def blocks_on_sublanes(zh_ref, zl_ref, hi_ref, lo_ref, y_ref):
    def body(j, carry):
        zh = jnp.concatenate([zh_ref[j, 0], zh_ref[j, 1]], axis=1)
        zl = jnp.concatenate([zl_ref[j, 0], zl_ref[j, 1]], axis=1)
        brh, bih = matrix(hi_ref, j, 0), matrix(hi_ref, j, 1)
        brl, bil = matrix(lo_ref, j, 0), matrix(lo_ref, j, 1)
        tr = dot(brh, zh) + dot(brl, zh) + dot(brh, zl)
        ti = dot(bih, zh) + dot(bil, zh) + dot(bih, zl)
        y_ref[j, 0] = tr[:, :LANES] - ti[:, LANES:]
        y_ref[j, 1] = tr[:, LANES:] + ti[:, :LANES]
        return carry

    lax.fori_loop(0, RADIX, body, 0)


def first_kernel(
    screens_ref,
    prof_ref,
    hi_hbm,
    lo_hbm,
    out_hbm,
    out_ref,
    s_ref,
    e_ref,
    hi_ref,
    lo_ref,
    cs_ref,
    zh_ref,
    zl_ref,
    y_ref,
    t_ref,
    screen_sems,
    table_sems,
    out_sems,
):
    m = lax.axis_index("modes")
    r = lax.axis_index("rows")
    rows = pl.ds(pl.multiple_of(m * 16, 16), 16)

    def screen_copy(k):
        return pltpu.make_async_copy(
            screens_ref.at[k, rows, :], s_ref.at[k], screen_sems.at[k]
        )

    def table_copies(t):
        return [
            pltpu.make_async_copy(hi_hbm.at[t], hi_ref.at[t], table_sems.at[0, t]),
            pltpu.make_async_copy(lo_hbm.at[t], lo_ref.at[t], table_sems.at[1, t]),
        ]

    for k in range(2):
        screen_copy(k).start()
    for j in range(RADIX):
        for copy in table_copies((RADIX - j) % RADIX):
            copy.start()

    cell = lax.broadcasted_iota(jnp.int32, (16, LANES), 0) + (r * 64 + m * 16)
    coord = (cell.astype(jnp.float32) - (N / 2 - 0.5)) / (N / 8)
    envelope = jnp.exp(-coord * coord) * AMPLITUDE
    screen_copy(0).wait()

    def screens(t, carry):
        lanes = pl.ds(pl.multiple_of(t * LANES, LANES), LANES)
        sine, cosine = sincos(s_ref[0, :, lanes])
        cs_ref[0, t] = cosine * envelope
        cs_ref[1, t] = sine * envelope
        return carry

    lax.fori_loop(0, 16, screens, 0, unroll=4)

    def forward(i, carry):
        b, h = i // 2, i % 2
        xs = []
        for q in range(RADIX):
            at = pl.ds(pl.multiple_of(q * BLOCK + h * LANES, LANES), LANES)
            weight = prof_ref[b, :, at]
            xs.append((cs_ref[0, q * 2 + h] * weight, cs_ref[1, q * 2 + h] * weight))
        for j, pair in enumerate(butterfly(xs)):
            for c in range(2):
                at = pl.ds(pl.multiple_of(c * 64 + b * 16, 16), 16)
                high, low = split(pair[c])
                zh_ref[j, h, at, :] = high
                zl_ref[j, h, at, :] = low
        return carry

    lax.fori_loop(0, 8, forward, 0, unroll=2)

    def wait(t):
        for copy in table_copies(t):
            copy.wait()

    blocks_on_lanes(64, zh_ref, zl_ref, hi_ref, lo_ref, y_ref, wait)

    def backward(i, carry):
        b, h = i // 2, i % 2
        at = pl.ds(pl.multiple_of(b * 16, 16), 16)
        ys = [(y_ref[j, 0, h, at, :], y_ref[j, 1, h, at, :]) for j in range(RADIX)]
        for q, pair in enumerate(unbutterfly(ys)):
            t_ref[q * 2 + h, b] = pair[0]
            t_ref[q * 2 + h, 4 + b] = pair[1]
        return carry

    lax.fori_loop(0, 8, backward, 0, unroll=2)
    screen_copy(1).wait()

    def lines(t, carry):
        lanes = pl.ds(pl.multiple_of(t * LANES, LANES), LANES)
        e_ref[pl.ds(pl.multiple_of(t * 16, 16), 16), :] = s_ref[1, :, lanes]
        return carry

    lax.fori_loop(0, 16, lines, 0, unroll=4)
    for t in range(0, 16, 4):
        values = [e_ref[pl.ds(t * 16 + g, 8, stride=8), :] for g in range(8)]
        for k, value in enumerate(swap_groups(values)):
            for u in range(4):
                at = ((t + u) * 8 + k) * MSG + 16
                out_ref[at : at + 2, :] = value[2 * u : 2 * u + 2, :]

    def sending(t):
        at = pl.ds(pl.multiple_of(t * (8 * MSG), 8), 8 * MSG)
        return pltpu.make_async_copy(out_ref.at[at, :], out_hbm.at[at, :], out_sems.at[t])

    def pack(t, carry):
        for k, value in enumerate(swap_groups([t_ref[t, k] for k in range(8)])):
            out_ref[pl.ds((t * 8 + k) * MSG, 16), :] = value
        sending(t).start()
        return carry

    lax.fori_loop(0, 16, pack, 0, unroll=4)
    for t in range(16):
        sending(t).wait()


def second_kernel(
    in_ref, hi_ref, lo_ref, out_hbm, p_ref, e_ref, zh_ref, zl_ref, y_ref, out_ref, sems
):
    groups = lane_groups((8, LANES))

    def gather(p, carry):
        for u in range(8):
            p_ref[pl.ds(p * 16 + u * 2, 2), :] = in_ref[pl.ds(p * (8 * MSG) + u * MSG + 16, 2), :]
        return carry

    lax.fori_loop(0, 16, gather, 0, unroll=4)

    def phases(p, carry):
        packed = p_ref[pl.ds(pl.multiple_of(p * 8, 8), 8), :]
        sine, cosine = sincos(packed)
        for c, value in enumerate((cosine, sine)):
            level = [value]
            for step in (4, 2, 1):
                keep = (groups & step) == 0
                following = []
                for value in level:
                    moved = pltpu.roll(value, step * GROUP, 1)
                    following.append(jnp.where(keep, value, moved))
                    following.append(jnp.where(keep, moved, value))
                level = following
            for k in range(8):
                e_ref[c, pl.ds(p * 64 + k, 8, stride=8), :] = level[k]
        return carry

    lax.fori_loop(0, 32, phases, 0, unroll=4)
    left = lax.broadcasted_iota(jnp.int32, (16, LANES), 1) < 64
    line = lax.broadcasted_iota(jnp.int32, (16, LANES), 0).astype(jnp.float32)
    line = (line - (N / 2 - 0.5)) * (2.0 / (N / 8))

    def store(at, pairs):
        for j, pair in enumerate(pairs):
            for c in range(2):
                high, low = split(pair[c])
                zh_ref[j, c, at, :] = high
                zl_ref[j, c, at, :] = low

    def load(at):
        return unbutterfly([(y_ref[j, 0, at, :], y_ref[j, 1, at, :]) for j in range(RADIX)])

    def forward(s, carry):
        start = (s * 16).astype(jnp.float32) * (2.0 / (N / 8))
        xs = []
        for q in range(RADIX):
            value = in_ref[pl.ds((s + q * 16) * MSG, 16), :]
            moved = pltpu.roll(value, 64, 1)
            factor = jnp.where(left, 1.0, line + (start + q * BLOCK * (2.0 / (N / 8))))
            xs.append((jnp.where(left, value, moved) * factor, jnp.where(left, moved, value) * factor))
        store(pl.ds(pl.multiple_of(s * 16, 16), 16), butterfly(xs))
        return carry

    lax.fori_loop(0, 16, forward, 0, unroll=2)
    blocks_on_sublanes(zh_ref, zl_ref, hi_ref, lo_ref, y_ref)

    def middle(s, carry):
        at = pl.ds(pl.multiple_of(s * 16, 16), 16)
        xs = []
        for q, (re, im) in enumerate(load(at)):
            here = pl.ds(pl.multiple_of(s * 16 + q * BLOCK, 16), 16)
            cosine, sine = e_ref[0, here, :], e_ref[1, here, :]
            xs.append((re * cosine - im * sine, re * sine + im * cosine))
        store(at, butterfly(xs))
        return carry

    lax.fori_loop(0, 16, middle, 0, unroll=2)
    blocks_on_sublanes(zh_ref, zl_ref, hi_ref, lo_ref, y_ref)

    def sending(s):
        return pltpu.make_async_copy(out_ref.at[:, s], out_hbm.at[:, s], sems.at[s])

    def backward(s, carry):
        at = pl.ds(pl.multiple_of(s * 16, 16), 16)
        for q, (re, im) in enumerate(load(at)):
            out_ref[q, s, 0:16, :] = re
            out_ref[q, s, 16:32, :] = im
        sending(s).start()
        return carry

    lax.fori_loop(0, 16, backward, 0, unroll=2)
    for s in range(16):
        sending(s).wait()


def third_kernel(
    in_hbm, weight_ref, hi_ref, lo_ref, out0, out1, out2, out3,
    x_ref, t_ref, zh_ref, zl_ref, y_ref, i_ref, sems,
):
    m = lax.axis_index("modes")

    def arrival(t):
        return pltpu.make_async_copy(in_hbm.at[pl.ds(t * 8, 8)], x_ref.at[pl.ds(t * 8, 8)], sems.at[t])

    for t in range(16):
        arrival(t).start()

    def unpack(t, carry):
        arrival(t).wait()
        for c in range(2):
            values = [x_ref[t * 8 + s, c * 16 : c * 16 + 16, :] for s in range(8)]
            for k, value in enumerate(swap_groups(values)):
                t_ref[t, c, k] = value
        return carry

    lax.fori_loop(0, 16, unpack, 0, unroll=2)

    def forward(i, carry):
        mode, h = i // 2, i % 2
        xs = [(t_ref[q * 2 + h, 0, mode], t_ref[q * 2 + h, 1, mode]) for q in range(RADIX)]
        for j, pair in enumerate(butterfly(xs)):
            for c in range(2):
                at = pl.ds(pl.multiple_of(c * 128 + mode * 16, 16), 16)
                high, low = split(pair[c])
                zh_ref[j, h, at, :] = high
                zl_ref[j, h, at, :] = low
        return carry

    lax.fori_loop(0, 16, forward, 0, unroll=2)
    blocks_on_lanes(128, zh_ref, zl_ref, hi_ref, lo_ref, y_ref)
    for t in range(16):
        i_ref[t] = jnp.zeros((16, LANES), jnp.float32)

    def backward(i, carry):
        mode, h = i // 2, i % 2
        at = pl.ds(pl.multiple_of(mode * 16, 16), 16)
        weight = weight_ref[jnp.bitwise_xor(m, mode // 2), mode % 2]
        ys = [(y_ref[j, 0, h, at, :], y_ref[j, 1, h, at, :]) for j in range(RADIX)]
        for q, (re, im) in enumerate(unbutterfly(ys)):
            i_ref[q * 2 + h] += weight * (re * re + im * im)
        return carry

    lax.fori_loop(0, 16, backward, 0, unroll=2)
    for k, out_ref in enumerate((out0, out1, out2, out3)):
        owner = jnp.bitwise_xor(m, k)
        for t in range(4):
            out_ref[:, t * LANES : (t + 1) * LANES] = i_ref[owner * 4 + t]


def last_kernel(in0, in1, in2, in3, out_ref):
    m = lax.axis_index("modes")
    for k, in_ref in enumerate((in0, in1, in2, in3)):
        row = pl.multiple_of(jnp.bitwise_xor(m, k) * 16, 16)
        out_ref[pl.ds(row, 16), :] = in_ref[...]


def f32(*shape):
    return jax.ShapeDtypeStruct(shape, jnp.float32)


def exchange(value):
    return lax.all_to_all(value, BOTH, split_axis=0, concat_axis=0, tiled=True)


def partner(value, k):
    return lax.ppermute(value, "modes", [(i, i ^ k) for i in range(4)])


def shards(screens, weights):
    high, low = (jnp.asarray(table) for table in block_tables())
    profiles = jnp.asarray(profile_table())
    vmem = pl.BlockSpec(memory_space=pltpu.VMEM)
    smem = pl.BlockSpec(memory_space=pltpu.SMEM)
    hbm = pl.BlockSpec(memory_space=pltpu.HBM)
    dma = pltpu.SemaphoreType.DMA
    table = pltpu.VMEM((RADIX, 2, 384, LANES), jnp.bfloat16)

    def scratch(*shape, kind=jnp.float32):
        return pltpu.VMEM(shape, kind)

    def halves(rows):
        return [scratch(RADIX, 2, rows, LANES, kind=jnp.bfloat16)] * 2

    mine = weights.reshape(1, 2)
    everyone = jnp.concatenate([mine] + [partner(mine, k) for k in (1, 2, 3)])

    sent = pl.pallas_call(
        first_kernel,
        out_shape=f32(128 * MSG, LANES),
        in_specs=[hbm, vmem, hbm, hbm],
        out_specs=hbm,
        scratch_shapes=[
            scratch(128 * MSG, LANES),
            scratch(2, 16, N),
            scratch(256, LANES),
            table,
            table,
            scratch(2, 16, 16, LANES),
            *halves(128),
            scratch(RADIX, 2, 2, 64, LANES),
            scratch(16, 8, 16, LANES),
            dma((2,)),
            dma((2, RADIX)),
            dma((16,)),
        ],
        name="first",
        compiler_params=params(60),
    )(screens, profiles, high, low)
    got = exchange(sent.reshape(128 * MSG, 1, LANES)).reshape(128 * MSG, LANES)

    sent = pl.pallas_call(
        second_kernel,
        out_shape=f32(RADIX, 16, 32, LANES),
        in_specs=[vmem] * 3,
        out_specs=hbm,
        scratch_shapes=[
            scratch(256, LANES),
            scratch(2, N, LANES),
            *halves(256),
            scratch(RADIX, 2, 256, LANES),
            scratch(RADIX, 16, 32, LANES),
            dma((16,)),
        ],
        name="second",
        compiler_params=params(48),
    )(got, high, low)
    got = exchange(sent.reshape(128, 32, LANES))

    pieces = pl.pallas_call(
        third_kernel,
        out_shape=[f32(16, 512)] * 4,
        in_specs=[hbm, smem, vmem, vmem],
        out_specs=[vmem] * 4,
        scratch_shapes=[
            scratch(128, 32, LANES),
            scratch(16, 2, 8, 16, LANES),
            *halves(256),
            scratch(RADIX, 2, 2, 128, LANES),
            scratch(16, 16, LANES),
            dma((16,)),
        ],
        name="third",
        compiler_params=params(40),
    )(got, everyone, high, low)
    pieces = [pieces[0]] + [partner(pieces[k], k) for k in (1, 2, 3)]

    return pl.pallas_call(
        last_kernel,
        out_shape=f32(64, 512),
        in_specs=[vmem] * 4,
        out_specs=vmem,
        name="last",
        compiler_params=params(24),
    )(*pieces)


def solution(mesh):
    return jax.shard_map(
        shards,
        mesh=mesh,
        in_specs=(P(None, "rows", None), P("modes")),
        out_specs=P("rows", "modes"),
        check_vma=False,
    )
```

time: 125 us -> 102 us (0.82)
  Pallas kernels: 49.6 us -> 29.2 us
  local copies, waits for them, and re-layouts: 1.93 us -> 0.02 us
  blocking collectives: 33.7 us -> 32.2 us
    pallas_call x3, Pallas kernels: 48.2 us -> 28.5 us  [the longest x1 11.8 us: shards(): pl.pallas_call(second_kernel, out_shape=f32(RADIX, 16, 32, LANES), in_spe...]
    unnamed x10 -> x6, local copies, waits for them, and re-layouts: 1.93 us -> 0.02 us
    all_to_all x1, blocking collectives: 33.7 us -> 32.2 us  [exchange(): return lax.all_to_all(value, BOTH, split_axis=0, concat_axis=0, tiled=True)]
  transfers between devices with their start and end apart: 7 -> 7, of which waited for: 4 -> 5; matrix products, arithmetic and copies ran while one was open for 0% -> 0% of each run, Pallas kernels for 0% -> 0%
where the time goes in v1:
time: 102 us; the launch traced here: 101 us
  blocking collectives  32.2 us (32%)
  Pallas kernels  29.2 us (29%)
  waiting for transfers between devices  29.2 us (29%)
  starting transfers between devices  10.8 us (11%)
    all_to_all x1, blocking collectives, exchange(): return lax.all_to_all(value, BOTH, split_axis=0, concat_axis=0, tiled=True)  32.2 us
    all_to_all x1, waiting for transfers between devices, exchange(): return lax.all_to_all(value, BOTH, split_axis=0, concat_axis=0, tiled=True)  24.8 us
    pallas_call x1, Pallas kernels, shards(): pl.pallas_call(second_kernel, out_shape=f32(RADIX, 16, 32, LANES), in_spe...  11.8 us
    pallas_call x1, Pallas kernels, shards(): pl.pallas_call(third_kernel, out_shape=[f32(16, 512)] * 4, in_specs=[hbm,...  8.71 us
    pallas_call x1, Pallas kernels, shards(): pl.pallas_call(first_kernel, out_shape=f32(128 * MSG, LANES), in_specs=[h...  7.99 us
    ppermute x6, starting transfers between devices, partner(): return lax.ppermute(value, 'modes', [(i, i ^ k) for i in range(4)])  5.75 us
    all_to_all x1, starting transfers between devices, exchange(): return lax.all_to_all(value, BOTH, split_axis=0, concat_axis=0, tiled=True)  5.03 us
    ppermute x6, waiting for transfers between devices, partner(): return lax.ppermute(value, 'modes', [(i, i ^ k) for i in range(4)])  4.46 us
  transfers between devices with their start and end apart: 7, of which 5 were waited for; matrix products, arithmetic and copies ran while one was open for 0% of the time, Pallas kernels for 0%

profile of v1, /device:TPU:1, one launch (start us, length us, event | category | flops | bytes accessed | tf_op | source)
XLA Modules:
  0.0 101.5 jit_solution(11560501472634658724)
XLA Ops:
  0.0 0.0 copy-start.1
  0.0 8.0 %first.1 = f32[2304,128]{1,0:T(8,128)} custom-call(f32[2,64,2048]{2,1,0:T(8,128)} %screens_ref.1, f32[4,1,2048]{2,1,0:T(1,128)} %constant.8.clone.prof_ref, bf16[8,2,384,128]{3,2,1,0:T(8,128)(2,1)} %constant.6.clone.hi_hbm.hi_ref, bf16[8,2,384,128]{3,2,1,0:T(8,128)(2,1)} %constant.7.clone.lo_hbm.lo_ref), custom_call_target="tpu_custom_call" | custom-call | tf_op jit(solution)/shard_map/first/pallas_call | solution.py:473
  8.0 0.0 copy-start
  8.0 32.2 %all_to_all.10 = f32[2304,1,128]{2,1,0:T(1,128)S(1)} all-to-all(f32[2304,1,128]{2,1,0:T(1,128)} %bitcast.8), channel_id=1, replica_groups=mesh['modes'=4,'rows'=32] {'rows','modes'}, dimensions={0} | all-to-all | bytes 2359296 | tf_op jit(solution)/shard_map/all_to_all | solution.py:448
  40.2 0.0 copy-done.1
  40.2 0.0 copy-done
  40.2 11.8 %second.1 = f32[8,16,32,128]{3,2,1,0:T(8,128)} custom-call(f32[2304,128]{1,0:T(8,128)S(1)} %bitcast.6, bf16[8,2,384,128]{3,2,1,0:T(8,128)(2,1)S(1)} %copy-done, bf16[8,2,384,128]{3,2,1,0:T(8,128)(2,1)S(1)} %copy-done.1), custom_call_target="tpu_custom_call" | custom-call | tf_op jit(solution)/shard_map/second/pallas_call | solution.py:497
  52.0 0.0 copy-start.2
  52.0 5.0 %all-to-all-start.1 = ((f32[128,32,128]{2,1,0:T(8,128)}), f32[128,32,128]{2,1,0:T(8,128)}, u32[]{:S(2)}, u32[]{:S(2)}) async-start(f32[128,32,128]{2,1,0:T(8,128)} %bitcast.7), calls=%async_computation.1 | async-start | bytes 4194304 | tf_op jit(solution)/shard_map/all_to_all | solution.py:448
  57.1 0.0 copy-done.2
  57.1 2.0 %collective-permute-start.2 = (f32[1,2]{1,0:T(1,128)S(1)}, f32[1,2]{1,0:T(1,128)S(1)}, u32[]{:S(2)}, u32[]{:S(2)}) collective-permute-start(f32[1,2]{1,0:T(1,128)S(1)} %bitcast.9), channel_id=1, source_target_pairs={{0,96},{32,64},{64,32},{96,0},{1,97},{33,65},{65,33},{97,1},{2,98}... | collective-permute-start | bytes 32 | tf_op jit(solution)/shard_map/ppermute | solution.py:452
  59.1 0.7 collective-permute-start.1
  59.8 0.0 collective-permute-start
  59.8 2.0 %collective-permute-done.2 = f32[1,2]{1,0:T(1,128)S(1)} collective-permute-done((f32[1,2]{1,0:T(1,128)S(1)}, f32[1,2]{1,0:T(1,128)S(1)}, u32[]{:S(2)}, u32[]{:S(2)}) %collective-permute-start.2) | collective-permute-done | bytes 40 | tf_op jit(solution)/shard_map/ppermute | solution.py:452
  61.8 0.1 collective-permute-done.1
  61.9 0.0 collective-permute-done
  61.9 24.8 %all-to-all-done.1.in_hbm = f32[128,32,128]{2,1,0:T(8,128)} async-done(((f32[128,32,128]{2,1,0:T(8,128)}), f32[128,32,128]{2,1,0:T(8,128)}, u32[]{:S(2)}, u32[]{:S(2)}) %all-to-all-start.1) | async-done | bytes 2097184 | tf_op jit(solution)/shard_map/all_to_all | solution.py:448
  86.7 8.7 %third.1 = (f32[16,512]{1,0:T(8,128)S(1)}, f32[16,512]{1,0:T(8,128)S(1)}, f32[16,512]{1,0:T(8,128)S(1)}, f32[16,512]{1,0:T(8,128)S(1)}) custom-call(f32[128,32,128]{2,1,0:T(8,128)} %all-to-all-done.1.in_hbm, f32[4,2]{1,0:T(4,128)S(1)} %pad_maximum_fusion.weight_ref, bf16[8,2,384,128]{3,2,1,0:T(8,128)(2,1)S(1)} %copy-done, bf16[8,2,384,128]{3,2,1,0:T(8,128)(2,1)S(1)} %copy-done.1), custom_call_target="tpu_custom_call" | custom-call | tf_op jit(solution)/shard_map/third/pallas_call | solution.py:515
  95.4 1.3 %collective-permute-start.3 = (f32[16,512]{1,0:T(8,128)S(1)}, f32[16,512]{1,0:T(8,128)S(1)}, u32[]{:S(2)}, u32[]{:S(2)}) collective-permute-start(f32[16,512]{1,0:T(8,128)S(1)} %get-tuple-element.10), channel_id=1, source_target_pairs={{0,32},{32,0},{64,96},{96,64},{1,33},{33,1},{65,97},{97,65},{2,34}... | collective-permute-start | bytes 98312 | tf_op jit(solution)/shard_map/ppermute | solution.py:452
  96.7 0.5 collective-permute-start.4
  97.2 1.2 %collective-permute-start.5 = (f32[16,512]{1,0:T(8,128)S(1)}, f32[16,512]{1,0:T(8,128)S(1)}, u32[]{:S(2)}, u32[]{:S(2)}) collective-permute-start(f32[16,512]{1,0:T(8,128)S(1)} %get-tuple-element.12), channel_id=1, source_target_pairs={{0,96},{32,64},{64,32},{96,0},{1,97},{33,65},{65,33},{97,1},{2,98}... | collective-permute-start | bytes 98312 | tf_op jit(solution)/shard_map/ppermute | solution.py:452
  98.4 0.0 collective-permute-done.3.in1
  98.4 1.0 %collective-permute-done.4.in2 = f32[16,512]{1,0:T(8,128)S(1)} collective-permute-done((f32[16,512]{1,0:T(8,128)S(1)}, f32[16,512]{1,0:T(8,128)S(1)}, u32[]{:S(2)}, u32[]{:S(2)}) %collective-permute-start.4) | collective-permute-done | bytes 32800 | tf_op jit(solution)/shard_map/ppermute | solution.py:452
  99.5 1.3 %collective-permute-done.5.in3 = f32[16,512]{1,0:T(8,128)S(1)} collective-permute-done((f32[16,512]{1,0:T(8,128)S(1)}, f32[16,512]{1,0:T(8,128)S(1)}, u32[]{:S(2)}, u32[]{:S(2)}) %collective-permute-start.5) | collective-permute-done | bytes 32800 | tf_op jit(solution)/shard_map/ppermute | solution.py:452
  100.8 0.7 last.1
  (1 shorter events, 0.0 us)
Async XLA Ops:
  0.0 40.2 %copy-start.1 = (bf16[8,2,384,128]{3,2,1,0:T(8,128)(2,1)S(1)}, bf16[8,2,384,128]{3,2,1,0:T(8,128)(2,1)}, u32[]{:S(2)}) copy-start(bf16[8,2,384,128]{3,2,1,0:T(8,128)(2,1)} %constant.7.clone.lo_hbm.lo_ref) | copy-start | bytes 4718596
  8.0 32.2 %copy-start = (bf16[8,2,384,128]{3,2,1,0:T(8,128)(2,1)S(1)}, bf16[8,2,384,128]{3,2,1,0:T(8,128)(2,1)}, u32[]{:S(2)}) copy-start(bf16[8,2,384,128]{3,2,1,0:T(8,128)(2,1)} %constant.6.clone.hi_hbm.hi_ref) | copy-start | bytes 4718596
  52.0 5.1 %copy-start.2 = (f32[2]{0:T(128)S(1)}, f32[2]{0:T(128)}, u32[]{:S(2)}) copy-start(f32[2]{0:T(128)} %param.6) | copy-start | bytes 28
  52.0 34.6 %all-to-all-start.1 = ((f32[128,32,128]{2,1,0:T(8,128)}), f32[128,32,128]{2,1,0:T(8,128)}, u32[]{:S(2)}, u32[]{:S(2)}) async-start(f32[128,32,128]{2,1,0:T(8,128)} %bitcast.7), calls=%async_computation.1 | async-start | bytes 4194304 | tf_op jit(solution)/shard_map/all_to_all | solution.py:448
  57.1 4.7 %collective-permute-start.2 = (f32[1,2]{1,0:T(1,128)S(1)}, f32[1,2]{1,0:T(1,128)S(1)}, u32[]{:S(2)}, u32[]{:S(2)}) collective-permute-start(f32[1,2]{1,0:T(1,128)S(1)} %bitcast.9), channel_id=1, source_target_pairs={{0,96},{32,64},{64,32},{96,0},{1,97},{33,65},{65,33},{97,1},{2,98}... | collective-permute-start | bytes 32 | tf_op jit(solution)/shard_map/ppermute | solution.py:452
  59.1 2.8 %collective-permute-start.1 = (f32[1,2]{1,0:T(1,128)S(1)}, f32[1,2]{1,0:T(1,128)S(1)}, u32[]{:S(2)}, u32[]{:S(2)}) collective-permute-start(f32[1,2]{1,0:T(1,128)S(1)} %bitcast.10), channel_id=1, source_target_pairs={{0,64},{32,96},{64,0},{96,32},{1,65},{33,97},{65,1},{97,33},{2,66}... | collective-permute-start | bytes 32 | tf_op jit(solution)/shard_map/ppermute | solution.py:452
  59.8 2.1 %collective-permute-start = (f32[1,2]{1,0:T(1,128)S(1)}, f32[1,2]{1,0:T(1,128)S(1)}, u32[]{:S(2)}, u32[]{:S(2)}) collective-permute-start(f32[1,2]{1,0:T(1,128)S(1)} %bitcast.11), channel_id=1, source_target_pairs={{0,32},{32,0},{64,96},{96,64},{1,33},{33,1},{65,97},{97,65},{2,34}... | collective-permute-start | bytes 32 | tf_op jit(solution)/shard_map/ppermute | solution.py:452
  95.4 3.0 %collective-permute-start.3 = (f32[16,512]{1,0:T(8,128)S(1)}, f32[16,512]{1,0:T(8,128)S(1)}, u32[]{:S(2)}, u32[]{:S(2)}) collective-permute-start(f32[16,512]{1,0:T(8,128)S(1)} %get-tuple-element.10), channel_id=1, source_target_pairs={{0,32},{32,0},{64,96},{96,64},{1,33},{33,1},{65,97},{97,65},{2,34}... | collective-permute-start | bytes 98312 | tf_op jit(solution)/shard_map/ppermute | solution.py:452
  96.7 2.8 %collective-permute-start.4 = (f32[16,512]{1,0:T(8,128)S(1)}, f32[16,512]{1,0:T(8,128)S(1)}, u32[]{:S(2)}, u32[]{:S(2)}) collective-permute-start(f32[16,512]{1,0:T(8,128)S(1)} %get-tuple-element.11), channel_id=1, source_target_pairs={{0,64},{32,96},{64,0},{96,32},{1,65},{33,97},{65,1},{97,33},{2,66}... | collective-permute-start | bytes 98312 | tf_op jit(solution)/shard_map/ppermute | solution.py:452
  97.2 3.6 %collective-permute-start.5 = (f32[16,512]{1,0:T(8,128)S(1)}, f32[16,512]{1,0:T(8,128)S(1)}, u32[]{:S(2)}, u32[]{:S(2)}) collective-permute-start(f32[16,512]{1,0:T(8,128)S(1)} %get-tuple-element.12), channel_id=1, source_target_pairs={{0,96},{32,64},{64,32},{96,0},{1,97},{33,65},{65,33},{97,1},{2,98}... | collective-permute-start | bytes 98312 | tf_op jit(solution)/shard_map/ppermute | solution.py:452

commit v2 on v1

--- a/solution.py
+++ b/solution.py
@@ -117,13 +117,18 @@
     return lax.broadcasted_iota(jnp.int32, shape, 1) // GROUP
 
 
-def swap_groups(rows):
+def swap_groups(rows, before=True, after=True):
     groups = lane_groups(rows[0].shape)
-    rows = [rows[0]] + [pltpu.roll(rows[k], k * GROUP, 1) for k in range(1, 8)]
+    rows = list(rows)
+    if before:
+        rows = [rows[0]] + [pltpu.roll(rows[k], k * GROUP, 1) for k in range(1, 8)]
     for step in (1, 2, 4):
         moves = (groups & step) != 0
         rows = [jnp.where(moves, rows[(k + step) % 8], rows[k]) for k in range(8)]
-    return [rows[0]] + [pltpu.roll(rows[8 - k], LANES - k * GROUP, 1) for k in range(1, 8)]
+    rows = [rows[0]] + [rows[8 - k] for k in range(1, 8)]
+    if after:
+        rows = [rows[0]] + [pltpu.roll(rows[k], LANES - k * GROUP, 1) for k in range(1, 8)]
+    return rows
 
 
 def matrix(table_ref, j, part):
@@ -146,8 +151,9 @@
         wrh, wih = matrix(hi_ref, t, 0), matrix(hi_ref, t, 1)
         wrl, wil = matrix(lo_ref, t, 0), matrix(lo_ref, t, 1)
         both = jnp.concatenate([zh, zl], axis=0)
-        pr, pi = dot(both, wrh), dot(both, wih)
+        pr = dot(both, wrh)
         pr = pr[: 2 * half] + pr[2 * half :] + dot(zh, wrl)
+        pi = dot(both, wih)
         pi = pi[: 2 * half] + pi[2 * half :] + dot(zh, wil)
         re = pr[:half] - pi[half:]
         im = pi[:half] + pr[half:]
@@ -176,10 +182,11 @@
 
 def first_kernel(
     screens_ref,
-    prof_ref,
+    prof_hbm,
     hi_hbm,
     lo_hbm,
     out_hbm,
+    prof_ref,
     out_ref,
     s_ref,
     e_ref,
@@ -209,8 +216,10 @@
             pltpu.make_async_copy(lo_hbm.at[t], lo_ref.at[t], table_sems.at[1, t]),
         ]
 
-    for k in range(2):
-        screen_copy(k).start()
+    prof_copy = pltpu.make_async_copy(prof_hbm, prof_ref, screen_sems.at[2])
+    screen_copy(0).start()
+    prof_copy.start()
+    screen_copy(1).start()
     for j in range(RADIX):
         for copy in table_copies((RADIX - j) % RADIX):
             copy.start()
@@ -228,6 +237,7 @@
         return carry
 
     lax.fori_loop(0, 16, screens, 0, unroll=4)
+    prof_copy.wait()
 
     def forward(i, carry):
         b, h = i // 2, i % 2
@@ -282,7 +292,7 @@
         return pltpu.make_async_copy(out_ref.at[at, :], out_hbm.at[at, :], out_sems.at[t])
 
     def pack(t, carry):
-        for k, value in enumerate(swap_groups([t_ref[t, k] for k in range(8)])):
+        for k, value in enumerate(swap_groups([t_ref[t, k] for k in range(8)], after=False)):
             out_ref[pl.ds((t * 8 + k) * MSG, 16), :] = value
         sending(t).start()
         return carry
@@ -322,7 +332,8 @@
         return carry
 
     lax.fori_loop(0, 32, phases, 0, unroll=4)
-    left = lax.broadcasted_iota(jnp.int32, (16, LANES), 1) < 64
+    turn = (lax.axis_index("rows") * 4 + lax.axis_index("modes")) % 8
+    left = ((lane_groups((16, LANES)) - turn + 8) & 7) < 4
     line = lax.broadcasted_iota(jnp.int32, (16, LANES), 0).astype(jnp.float32)
     line = (line - (N / 2 - 0.5)) * (2.0 / (N / 8))
 
@@ -395,7 +406,7 @@
         arrival(t).wait()
         for c in range(2):
             values = [x_ref[t * 8 + s, c * 16 : c * 16 + 16, :] for s in range(8)]
-            for k, value in enumerate(swap_groups(values)):
+            for k, value in enumerate(swap_groups(values, before=False)):
                 t_ref[t, c, k] = value
         return carry
 
@@ -420,7 +431,7 @@
     def backward(i, carry):
         mode, h = i // 2, i % 2
         at = pl.ds(pl.multiple_of(mode * 16, 16), 16)
-        weight = weight_ref[jnp.bitwise_xor(m, mode // 2), mode % 2]
+        weight = weight_ref[jnp.bitwise_xor(m, mode // 2) * 2 + mode % 2]
         ys = [(y_ref[j, 0, h, at, :], y_ref[j, 1, h, at, :]) for j in range(RADIX)]
         for q, (re, im) in enumerate(unbutterfly(ys)):
             i_ref[q * 2 + h] += weight * (re * re + im * im)
@@ -456,7 +467,6 @@
     high, low = (jnp.asarray(table) for table in block_tables())
     profiles = jnp.asarray(profile_table())
     vmem = pl.BlockSpec(memory_space=pltpu.VMEM)
-    smem = pl.BlockSpec(memory_space=pltpu.SMEM)
     hbm = pl.BlockSpec(memory_space=pltpu.HBM)
     dma = pltpu.SemaphoreType.DMA
     table = pltpu.VMEM((RADIX, 2, 384, LANES), jnp.bfloat16)
@@ -469,13 +479,15 @@
 
     mine = weights.reshape(1, 2)
     everyone = jnp.concatenate([mine] + [partner(mine, k) for k in (1, 2, 3)])
+    everyone = jnp.broadcast_to(everyone.reshape(8, 1, 1), (8, 1, LANES))
 
     sent = pl.pallas_call(
         first_kernel,
         out_shape=f32(128 * MSG, LANES),
-        in_specs=[hbm, vmem, hbm, hbm],
+        in_specs=[hbm] * 4,
         out_specs=hbm,
         scratch_shapes=[
+            scratch(4, 1, N),
             scratch(128 * MSG, LANES),
             scratch(2, 16, N),
             scratch(256, LANES),
@@ -485,7 +497,7 @@
             *halves(128),
             scratch(RADIX, 2, 2, 64, LANES),
             scratch(16, 8, 16, LANES),
-            dma((2,)),
+            dma((3,)),
             dma((2, RADIX)),
             dma((16,)),
         ],
@@ -515,7 +527,7 @@
     pieces = pl.pallas_call(
         third_kernel,
         out_shape=[f32(16, 512)] * 4,
-        in_specs=[hbm, smem, vmem, vmem],
+        in_specs=[hbm, vmem, vmem, vmem],
         out_specs=[vmem] * 4,
         scratch_shapes=[
             scratch(128, 32, LANES),

time: 102 us -> 98.8 us (0.969)
  Pallas kernels: 29.2 us -> 26.1 us
    pallas_call x1, Pallas kernels: 8.71 us -> 6.95 us  [shards(): pl.pallas_call(third_kernel, out_shape=[f32(16, 512)] * 4, in_specs=[hbm,...]
    pallas_call x1, Pallas kernels: 7.99 us -> 6.69 us  [shards(): pl.pallas_call(first_kernel, out_shape=f32(128 * MSG, LANES), in_specs=[h...]
where the time goes in v2:
time: 98.8 us; the launch traced here: 98.5 us
  blocking collectives  32.2 us (33%)
  waiting for transfers between devices  29.1 us (29%)
  Pallas kernels  26.1 us (26%)
  starting transfers between devices  10.8 us (11%)
    all_to_all x1, blocking collectives, exchange(): return lax.all_to_all(value, BOTH, split_axis=0, concat_axis=0, tiled=True)  32.2 us
    all_to_all x1, waiting for transfers between devices, exchange(): return lax.all_to_all(value, BOTH, split_axis=0, concat_axis=0, tiled=True)  24.7 us
    pallas_call x1, Pallas kernels, shards(): pl.pallas_call(second_kernel, out_shape=f32(RADIX, 16, 32, LANES), in_spe...  11.8 us
    pallas_call x1, Pallas kernels, shards(): pl.pallas_call(third_kernel, out_shape=[f32(16, 512)] * 4, in_specs=[hbm,...  6.95 us
    pallas_call x1, Pallas kernels, shards(): pl.pallas_call(first_kernel, out_shape=f32(128 * MSG, LANES), in_specs=[h...  6.69 us
    ppermute x6, starting transfers between devices, partner(): return lax.ppermute(value, 'modes', [(i, i ^ k) for i in range(4)])  5.75 us
    all_to_all x1, starting transfers between devices, exchange(): return lax.all_to_all(value, BOTH, split_axis=0, concat_axis=0, tiled=True)  5.04 us
    ppermute x6, waiting for transfers between devices, partner(): return lax.ppermute(value, 'modes', [(i, i ^ k) for i in range(4)])  4.46 us
  transfers between devices with their start and end apart: 7, of which 5 were waited for; matrix products, arithmetic and copies ran while one was open for 0% of the time, Pallas kernels for 0%

profile of v2, /device:TPU:1, one launch (start us, length us, event | category | flops | bytes accessed | tf_op | source)
XLA Modules:
  0.0 98.5 jit_solution(3408464367402096634)
XLA Ops:
  0.0 0.0 copy-start.1
  0.0 6.7 %first.1 = f32[2304,128]{1,0:T(8,128)} custom-call(f32[2,64,2048]{2,1,0:T(8,128)} %screens_ref.1, f32[4,1,2048]{2,1,0:T(1,128)} %constant.8.clone.prof_hbm, bf16[8,2,384,128]{3,2,1,0:T(8,128)(2,1)} %constant.6.clone.hi_hbm.hi_ref, bf16[8,2,384,128]{3,2,1,0:T(8,128)(2,1)} %constant.7.clone.lo_hbm.lo_ref), custom_call_target="tpu_custom_call" | custom-call | tf_op jit(solution)/shard_map/first/pallas_call | solution.py:484
  6.7 0.0 copy-start
  6.7 32.2 %all_to_all.10 = f32[2304,1,128]{2,1,0:T(1,128)S(1)} all-to-all(f32[2304,1,128]{2,1,0:T(1,128)} %bitcast.8), channel_id=1, replica_groups=mesh['modes'=4,'rows'=32] {'rows','modes'}, dimensions={0} | all-to-all | bytes 2359296 | tf_op jit(solution)/shard_map/all_to_all | solution.py:459
  38.9 0.0 copy-done.1
  38.9 0.0 copy-done
  38.9 11.8 %second.1 = f32[8,16,32,128]{3,2,1,0:T(8,128)} custom-call(f32[2304,128]{1,0:T(8,128)S(1)} %bitcast.6, bf16[8,2,384,128]{3,2,1,0:T(8,128)(2,1)S(1)} %copy-done, bf16[8,2,384,128]{3,2,1,0:T(8,128)(2,1)S(1)} %copy-done.1), custom_call_target="tpu_custom_call" | custom-call | tf_op jit(solution)/shard_map/second/pallas_call | solution.py:509
  50.7 0.0 copy-start.2
  50.7 5.0 %all-to-all-start.1 = ((f32[128,32,128]{2,1,0:T(8,128)}), f32[128,32,128]{2,1,0:T(8,128)}, u32[]{:S(2)}, u32[]{:S(2)}) async-start(f32[128,32,128]{2,1,0:T(8,128)} %bitcast.7), calls=%async_computation.1 | async-start | bytes 4194304 | tf_op jit(solution)/shard_map/all_to_all | solution.py:459
  55.8 0.0 copy-done.2
  55.8 2.0 %collective-permute-start.2 = (f32[1,2]{1,0:T(1,128)S(1)}, f32[1,2]{1,0:T(1,128)S(1)}, u32[]{:S(2)}, u32[]{:S(2)}) collective-permute-start(f32[1,2]{1,0:T(1,128)S(1)} %bitcast.9), channel_id=1, source_target_pairs={{0,96},{32,64},{64,32},{96,0},{1,97},{33,65},{65,33},{97,1},{2,98}... | collective-permute-start | bytes 32 | tf_op jit(solution)/shard_map/ppermute | solution.py:463
  57.8 0.7 collective-permute-start.1
  58.5 0.0 collective-permute-start
  58.5 2.0 %collective-permute-done.2 = f32[1,2]{1,0:T(1,128)S(1)} collective-permute-done((f32[1,2]{1,0:T(1,128)S(1)}, f32[1,2]{1,0:T(1,128)S(1)}, u32[]{:S(2)}, u32[]{:S(2)}) %collective-permute-start.2) | collective-permute-done | bytes 40 | tf_op jit(solution)/shard_map/ppermute | solution.py:463
  60.5 0.1 collective-permute-done.1
  60.6 0.0 collective-permute-done
  60.6 0.1 broadcast_in_dim.7
  60.7 24.7 %all-to-all-done.1.in_hbm = f32[128,32,128]{2,1,0:T(8,128)} async-done(((f32[128,32,128]{2,1,0:T(8,128)}), f32[128,32,128]{2,1,0:T(8,128)}, u32[]{:S(2)}, u32[]{:S(2)}) %all-to-all-start.1) | async-done | bytes 2097184 | tf_op jit(solution)/shard_map/all_to_all | solution.py:459
  85.4 0.1 broadcast_in_dim.8.weight_ref
  85.4 6.9 %third.1 = (f32[16,512]{1,0:T(8,128)S(1)}, f32[16,512]{1,0:T(8,128)S(1)}, f32[16,512]{1,0:T(8,128)S(1)}, f32[16,512]{1,0:T(8,128)S(1)}) custom-call(f32[128,32,128]{2,1,0:T(8,128)} %all-to-all-done.1.in_hbm, f32[8,1,128]{2,1,0:T(1,128)S(1)} %broadcast_in_dim.8.weight_ref, bf16[8,2,384,128]{3,2,1,0:T(8,128)(2,1)S(1)} %copy-done, ...), custom_call_target="tpu_custom_call" | custom-call | tf_op jit(solution)/shard_map/third/pallas_call | solution.py:527
  92.4 1.3 %collective-permute-start.3 = (f32[16,512]{1,0:T(8,128)S(1)}, f32[16,512]{1,0:T(8,128)S(1)}, u32[]{:S(2)}, u32[]{:S(2)}) collective-permute-start(f32[16,512]{1,0:T(8,128)S(1)} %get-tuple-element.10), channel_id=1, source_target_pairs={{0,32},{32,0},{64,96},{96,64},{1,33},{33,1},{65,97},{97,65},{2,34}... | collective-permute-start | bytes 98312 | tf_op jit(solution)/shard_map/ppermute | solution.py:463
  93.7 0.5 collective-permute-start.4
  94.2 1.2 %collective-permute-start.5 = (f32[16,512]{1,0:T(8,128)S(1)}, f32[16,512]{1,0:T(8,128)S(1)}, u32[]{:S(2)}, u32[]{:S(2)}) collective-permute-start(f32[16,512]{1,0:T(8,128)S(1)} %get-tuple-element.12), channel_id=1, source_target_pairs={{0,96},{32,64},{64,32},{96,0},{1,97},{33,65},{65,33},{97,1},{2,98}... | collective-permute-start | bytes 98312 | tf_op jit(solution)/shard_map/ppermute | solution.py:463
  95.4 0.0 collective-permute-done.3.in1
  95.4 1.0 %collective-permute-done.4.in2 = f32[16,512]{1,0:T(8,128)S(1)} collective-permute-done((f32[16,512]{1,0:T(8,128)S(1)}, f32[16,512]{1,0:T(8,128)S(1)}, u32[]{:S(2)}, u32[]{:S(2)}) %collective-permute-start.4) | collective-permute-done | bytes 32800 | tf_op jit(solution)/shard_map/ppermute | solution.py:463
  96.5 1.3 %collective-permute-done.5.in3 = f32[16,512]{1,0:T(8,128)S(1)} collective-permute-done((f32[16,512]{1,0:T(8,128)S(1)}, f32[16,512]{1,0:T(8,128)S(1)}, u32[]{:S(2)}, u32[]{:S(2)}) %collective-permute-start.5) | collective-permute-done | bytes 32800 | tf_op jit(solution)/shard_map/ppermute | solution.py:463
  97.8 0.7 last.1
  (1 shorter events, 0.0 us)
Async XLA Ops:
  0.0 38.9 %copy-start.1 = (bf16[8,2,384,128]{3,2,1,0:T(8,128)(2,1)S(1)}, bf16[8,2,384,128]{3,2,1,0:T(8,128)(2,1)}, u32[]{:S(2)}) copy-start(bf16[8,2,384,128]{3,2,1,0:T(8,128)(2,1)} %constant.7.clone.lo_hbm.lo_ref) | copy-start | bytes 4718596
  6.7 32.2 %copy-start = (bf16[8,2,384,128]{3,2,1,0:T(8,128)(2,1)S(1)}, bf16[8,2,384,128]{3,2,1,0:T(8,128)(2,1)}, u32[]{:S(2)}) copy-start(bf16[8,2,384,128]{3,2,1,0:T(8,128)(2,1)} %constant.6.clone.hi_hbm.hi_ref) | copy-start | bytes 4718596
  50.7 5.1 %copy-start.2 = (f32[2]{0:T(128)S(1)}, f32[2]{0:T(128)}, u32[]{:S(2)}) copy-start(f32[2]{0:T(128)} %param.6) | copy-start | bytes 28
  50.7 34.6 %all-to-all-start.1 = ((f32[128,32,128]{2,1,0:T(8,128)}), f32[128,32,128]{2,1,0:T(8,128)}, u32[]{:S(2)}, u32[]{:S(2)}) async-start(f32[128,32,128]{2,1,0:T(8,128)} %bitcast.7), calls=%async_computation.1 | async-start | bytes 4194304 | tf_op jit(solution)/shard_map/all_to_all | solution.py:459
  55.8 4.7 %collective-permute-start.2 = (f32[1,2]{1,0:T(1,128)S(1)}, f32[1,2]{1,0:T(1,128)S(1)}, u32[]{:S(2)}, u32[]{:S(2)}) collective-permute-start(f32[1,2]{1,0:T(1,128)S(1)} %bitcast.9), channel_id=1, source_target_pairs={{0,96},{32,64},{64,32},{96,0},{1,97},{33,65},{65,33},{97,1},{2,98}... | collective-permute-start | bytes 32 | tf_op jit(solution)/shard_map/ppermute | solution.py:463
  57.8 2.8 %collective-permute-start.1 = (f32[1,2]{1,0:T(1,128)S(1)}, f32[1,2]{1,0:T(1,128)S(1)}, u32[]{:S(2)}, u32[]{:S(2)}) collective-permute-start(f32[1,2]{1,0:T(1,128)S(1)} %bitcast.10), channel_id=1, source_target_pairs={{0,64},{32,96},{64,0},{96,32},{1,65},{33,97},{65,1},{97,33},{2,66}... | collective-permute-start | bytes 32 | tf_op jit(solution)/shard_map/ppermute | solution.py:463
  58.5 2.1 %collective-permute-start = (f32[1,2]{1,0:T(1,128)S(1)}, f32[1,2]{1,0:T(1,128)S(1)}, u32[]{:S(2)}, u32[]{:S(2)}) collective-permute-start(f32[1,2]{1,0:T(1,128)S(1)} %bitcast.11), channel_id=1, source_target_pairs={{0,32},{32,0},{64,96},{96,64},{1,33},{33,1},{65,97},{97,65},{2,34}... | collective-permute-start | bytes 32 | tf_op jit(solution)/shard_map/ppermute | solution.py:463
  92.4 3.0 %collective-permute-start.3 = (f32[16,512]{1,0:T(8,128)S(1)}, f32[16,512]{1,0:T(8,128)S(1)}, u32[]{:S(2)}, u32[]{:S(2)}) collective-permute-start(f32[16,512]{1,0:T(8,128)S(1)} %get-tuple-element.10), channel_id=1, source_target_pairs={{0,32},{32,0},{64,96},{96,64},{1,33},{33,1},{65,97},{97,65},{2,34}... | collective-permute-start | bytes 98312 | tf_op jit(solution)/shard_map/ppermute | solution.py:463
  93.7 2.8 %collective-permute-start.4 = (f32[16,512]{1,0:T(8,128)S(1)}, f32[16,512]{1,0:T(8,128)S(1)}, u32[]{:S(2)}, u32[]{:S(2)}) collective-permute-start(f32[16,512]{1,0:T(8,128)S(1)} %get-tuple-element.11), channel_id=1, source_target_pairs={{0,64},{32,96},{64,0},{96,32},{1,65},{33,97},{65,1},{97,33},{2,66}... | collective-permute-start | bytes 98312 | tf_op jit(solution)/shard_map/ppermute | solution.py:463
  94.2 3.6 %collective-permute-start.5 = (f32[16,512]{1,0:T(8,128)S(1)}, f32[16,512]{1,0:T(8,128)S(1)}, u32[]{:S(2)}, u32[]{:S(2)}) collective-permute-start(f32[16,512]{1,0:T(8,128)S(1)} %get-tuple-element.12), channel_id=1, source_target_pairs={{0,96},{32,64},{64,32},{96,0},{1,97},{33,65},{65,33},{97,1},{2,98}... | collective-permute-start | bytes 98312 | tf_op jit(solution)/shard_map/ppermute | solution.py:463

commit v3 on v2

--- a/solution.py
+++ b/solution.py
@@ -141,43 +141,41 @@
     return jnp.dot(left, right, preferred_element_type=jnp.float32)
 
 
-def blocks_on_lanes(half, zh_ref, zl_ref, hi_ref, lo_ref, y_ref, wait=None):
-    def body(j, carry):
-        t = lax.rem(RADIX - j, RADIX)
-        if wait is not None:
-            wait(t)
-        zh = jnp.concatenate([zh_ref[j, 0], zh_ref[j, 1]], axis=1)
-        zl = jnp.concatenate([zl_ref[j, 0], zl_ref[j, 1]], axis=1)
-        wrh, wih = matrix(hi_ref, t, 0), matrix(hi_ref, t, 1)
-        wrl, wil = matrix(lo_ref, t, 0), matrix(lo_ref, t, 1)
-        both = jnp.concatenate([zh, zl], axis=0)
-        pr = dot(both, wrh)
-        pr = pr[: 2 * half] + pr[2 * half :] + dot(zh, wrl)
-        pi = dot(both, wih)
-        pi = pi[: 2 * half] + pi[2 * half :] + dot(zh, wil)
-        re = pr[:half] - pi[half:]
-        im = pi[:half] + pr[half:]
-        for h in range(2):
-            y_ref[j, 0, h] = re[:, h * LANES : (h + 1) * LANES]
-            y_ref[j, 1, h] = im[:, h * LANES : (h + 1) * LANES]
-        return carry
-
-    lax.fori_loop(0, RADIX, body, 0)
-
-
-def blocks_on_sublanes(zh_ref, zl_ref, hi_ref, lo_ref, y_ref):
-    def body(j, carry):
-        zh = jnp.concatenate([zh_ref[j, 0], zh_ref[j, 1]], axis=1)
-        zl = jnp.concatenate([zl_ref[j, 0], zl_ref[j, 1]], axis=1)
-        brh, bih = matrix(hi_ref, j, 0), matrix(hi_ref, j, 1)
-        brl, bil = matrix(lo_ref, j, 0), matrix(lo_ref, j, 1)
-        tr = dot(brh, zh) + dot(brl, zh) + dot(brh, zl)
-        ti = dot(bih, zh) + dot(bil, zh) + dot(bih, zl)
-        y_ref[j, 0] = tr[:, :LANES] - ti[:, LANES:]
-        y_ref[j, 1] = tr[:, LANES:] + ti[:, :LANES]
-        return carry
-
-    lax.fori_loop(0, RADIX, body, 0)
+def block_on_lanes(j, half, zh_ref, zl_ref, hi_ref, lo_ref, y_ref):
+    t = lax.rem(RADIX - j, RADIX)
+    zh = jnp.concatenate([zh_ref[j, 0], zh_ref[j, 1]], axis=1)
+    zl = jnp.concatenate([zl_ref[j, 0], zl_ref[j, 1]], axis=1)
+    wrh, wih = matrix(hi_ref, t, 0), matrix(hi_ref, t, 1)
+    wrl, wil = matrix(lo_ref, t, 0), matrix(lo_ref, t, 1)
+    both = jnp.concatenate([zh, zl], axis=0)
+    pr = dot(both, wrh)
+    pr = pr[: 2 * half] + pr[2 * half :] + dot(zh, wrl)
+    pi = dot(both, wih)
+    pi = pi[: 2 * half] + pi[2 * half :] + dot(zh, wil)
+    re = pr[:half] - pi[half:]
+    im = pi[:half] + pr[half:]
+    for h in range(2):
+        y_ref[j, 0, h] = re[:, h * LANES : (h + 1) * LANES]
+        y_ref[j, 1, h] = im[:, h * LANES : (h + 1) * LANES]
+
+
+def block_on_sublanes(j, zh_ref, zl_ref, hi_ref, lo_ref, y_ref):
+    zh = jnp.concatenate([zh_ref[j, 0], zh_ref[j, 1]], axis=1)
+    zl = jnp.concatenate([zl_ref[j, 0], zl_ref[j, 1]], axis=1)
+    brh, bih = matrix(hi_ref, j, 0), matrix(hi_ref, j, 1)
+    brl, bil = matrix(lo_ref, j, 0), matrix(lo_ref, j, 1)
+    tr = dot(brh, zh) + dot(brl, zh) + dot(brh, zl)
+    ti = dot(bih, zh) + dot(bil, zh) + dot(bih, zl)
+    y_ref[j, 0] = tr[:, :LANES] - ti[:, LANES:]
+    y_ref[j, 1] = tr[:, LANES:] + ti[:, :LANES]
+
+
+def loop(count, body, unroll=1):
+    def step(i, carry):
+        body(i)
+        return carry
+
+    lax.fori_loop(0, count, step, 0, unroll=unroll)
 
 
 def first_kernel(
@@ -256,11 +254,28 @@
 
     lax.fori_loop(0, 8, forward, 0, unroll=2)
 
-    def wait(t):
-        for copy in table_copies(t):
-            copy.wait()
-
-    blocks_on_lanes(64, zh_ref, zl_ref, hi_ref, lo_ref, y_ref, wait)
+    screen_copy(1).wait()
+
+    def lines(t, carry):
+        lanes = pl.ds(pl.multiple_of(t * LANES, LANES), LANES)
+        e_ref[pl.ds(pl.multiple_of(t * 16, 16), 16), :] = s_ref[1, :, lanes]
+        return carry
+
+    lax.fori_loop(0, 16, lines, 0, unroll=4)
+
+    def products(p):
+        for j in (2 * p, 2 * p + 1):
+            for copy in table_copies(lax.rem(RADIX - j, RADIX)):
+                copy.wait()
+        for j in (2 * p, 2 * p + 1):
+            block_on_lanes(j, 64, zh_ref, zl_ref, hi_ref, lo_ref, y_ref)
+        values = [e_ref[pl.ds(p * 64 + g, 8, stride=8), :] for g in range(8)]
+        for k, value in enumerate(swap_groups(values)):
+            for u in range(4):
+                at = pl.ds(p * (32 * MSG) + ((u * 8 + k) * MSG + 16), 2)
+                out_ref[at, :] = value[2 * u : 2 * u + 2, :]
+
+    loop(4, products)
 
     def backward(i, carry):
         b, h = i // 2, i % 2
@@ -272,21 +287,6 @@
         return carry
 
     lax.fori_loop(0, 8, backward, 0, unroll=2)
-    screen_copy(1).wait()
-
-    def lines(t, carry):
-        lanes = pl.ds(pl.multiple_of(t * LANES, LANES), LANES)
-        e_ref[pl.ds(pl.multiple_of(t * 16, 16), 16), :] = s_ref[1, :, lanes]
-        return carry
-
-    lax.fori_loop(0, 16, lines, 0, unroll=4)
-    for t in range(0, 16, 4):
-        values = [e_ref[pl.ds(t * 16 + g, 8, stride=8), :] for g in range(8)]
-        for k, value in enumerate(swap_groups(values)):
-            for u in range(4):
-                at = ((t + u) * 8 + k) * MSG + 16
-                out_ref[at : at + 2, :] = value[2 * u : 2 * u + 2, :]
-
     def sending(t):
         at = pl.ds(pl.multiple_of(t * (8 * MSG), 8), 8 * MSG)
         return pltpu.make_async_copy(out_ref.at[at, :], out_hbm.at[at, :], out_sems.at[t])
@@ -314,7 +314,7 @@
 
     lax.fori_loop(0, 16, gather, 0, unroll=4)
 
-    def phases(p, carry):
+    def phases(p):
         packed = p_ref[pl.ds(pl.multiple_of(p * 8, 8), 8), :]
         sine, cosine = sincos(packed)
         for c, value in enumerate((cosine, sine)):
@@ -329,9 +329,7 @@
                 level = following
             for k in range(8):
                 e_ref[c, pl.ds(p * 64 + k, 8, stride=8), :] = level[k]
-        return carry
-
-    lax.fori_loop(0, 32, phases, 0, unroll=4)
+
     turn = (lax.axis_index("rows") * 4 + lax.axis_index("modes")) % 8
     left = ((lane_groups((16, LANES)) - turn + 8) & 7) < 4
     line = lax.broadcasted_iota(jnp.int32, (16, LANES), 0).astype(jnp.float32)
@@ -359,7 +357,13 @@
         return carry
 
     lax.fori_loop(0, 16, forward, 0, unroll=2)
-    blocks_on_sublanes(zh_ref, zl_ref, hi_ref, lo_ref, y_ref)
+
+    def products(j):
+        block_on_sublanes(j, zh_ref, zl_ref, hi_ref, lo_ref, y_ref)
+        for u in range(4):
+            phases(j * 4 + u)
+
+    loop(RADIX, products)
 
     def middle(s, carry):
         at = pl.ds(pl.multiple_of(s * 16, 16), 16)
@@ -372,7 +376,7 @@
         return carry
 
     lax.fori_loop(0, 16, middle, 0, unroll=2)
-    blocks_on_sublanes(zh_ref, zl_ref, hi_ref, lo_ref, y_ref)
+    loop(RADIX, lambda j: block_on_sublanes(j, zh_ref, zl_ref, hi_ref, lo_ref, y_ref))
 
     def sending(s):
         return pltpu.make_async_copy(out_ref.at[:, s], out_hbm.at[:, s], sems.at[s])
@@ -412,7 +416,10 @@
 
     lax.fori_loop(0, 16, unpack, 0, unroll=2)
 
-    def forward(i, carry):
+    for t in range(16):
+        i_ref[t] = jnp.zeros((16, LANES), jnp.float32)
+
+    def forward(i):
         mode, h = i // 2, i % 2
         xs = [(t_ref[q * 2 + h, 0, mode], t_ref[q * 2 + h, 1, mode]) for q in range(RADIX)]
         for j, pair in enumerate(butterfly(xs)):
@@ -421,23 +428,18 @@
                 high, low = split(pair[c])
                 zh_ref[j, h, at, :] = high
                 zl_ref[j, h, at, :] = low
-        return carry
-
-    lax.fori_loop(0, 16, forward, 0, unroll=2)
-    blocks_on_lanes(128, zh_ref, zl_ref, hi_ref, lo_ref, y_ref)
-    for t in range(16):
-        i_ref[t] = jnp.zeros((16, LANES), jnp.float32)
-
-    def backward(i, carry):
+
+    def backward(i):
         mode, h = i // 2, i % 2
         at = pl.ds(pl.multiple_of(mode * 16, 16), 16)
         weight = weight_ref[jnp.bitwise_xor(m, mode // 2) * 2 + mode % 2]
         ys = [(y_ref[j, 0, h, at, :], y_ref[j, 1, h, at, :]) for j in range(RADIX)]
         for q, (re, im) in enumerate(unbutterfly(ys)):
             i_ref[q * 2 + h] += weight * (re * re + im * im)
-        return carry
-
-    lax.fori_loop(0, 16, backward, 0, unroll=2)
+
+    loop(16, forward, unroll=2)
+    loop(RADIX, lambda j: block_on_lanes(j, 128, zh_ref, zl_ref, hi_ref, lo_ref, y_ref))
+    loop(16, backward, unroll=2)
     for k, out_ref in enumerate((out0, out1, out2, out3)):
         owner = jnp.bitwise_xor(m, k)
         for t in range(4):

time: 98.8 us -> 96 us (0.972)
  Pallas kernels: 26.1 us -> 23.3 us
    pallas_call x1, Pallas kernels: 11.8 us -> 9.88 us  [shards(): pl.pallas_call(second_kernel, out_shape=f32(RADIX, 16, 32, LANES), in_spe...]
where the time goes in v3:
time: 96 us; the launch traced here: 95.7 us
  blocking collectives  32.2 us (34%)
  waiting for transfers between devices  29.1 us (30%)
  Pallas kernels  23.3 us (24%)
  starting transfers between devices  10.8 us (11%)
    all_to_all x1, blocking collectives, exchange(): return lax.all_to_all(value, BOTH, split_axis=0, concat_axis=0, tiled=True)  32.2 us
    all_to_all x1, waiting for transfers between devices, exchange(): return lax.all_to_all(value, BOTH, split_axis=0, concat_axis=0, tiled=True)  24.7 us
    pallas_call x1, Pallas kernels, shards(): pl.pallas_call(second_kernel, out_shape=f32(RADIX, 16, 32, LANES), in_spe...  9.88 us
    pallas_call x1, Pallas kernels, shards(): pl.pallas_call(third_kernel, out_shape=[f32(16, 512)] * 4, in_specs=[hbm,...  6.94 us
    pallas_call x1, Pallas kernels, shards(): pl.pallas_call(first_kernel, out_shape=f32(128 * MSG, LANES), in_specs=[h...  5.85 us
    ppermute x6, starting transfers between devices, partner(): return lax.ppermute(value, 'modes', [(i, i ^ k) for i in range(4)])  5.75 us
    all_to_all x1, starting transfers between devices, exchange(): return lax.all_to_all(value, BOTH, split_axis=0, concat_axis=0, tiled=True)  5.03 us
    ppermute x6, waiting for transfers between devices, partner(): return lax.ppermute(value, 'modes', [(i, i ^ k) for i in range(4)])  4.46 us
  transfers between devices with their start and end apart: 7, of which 5 were waited for; matrix products, arithmetic and copies ran while one was open for 0% of the time, Pallas kernels for 0%

profile of v3, /device:TPU:1, one launch (start us, length us, event | category | flops | bytes accessed | tf_op | source)
XLA Modules:
  0.0 95.7 jit_solution(13032446261343241439)
XLA Ops:
  0.0 0.0 copy-start.1
  0.0 5.9 %first.1 = f32[2304,128]{1,0:T(8,128)} custom-call(f32[2,64,2048]{2,1,0:T(8,128)} %screens_ref.1, f32[4,1,2048]{2,1,0:T(1,128)} %constant.8.clone.prof_hbm, bf16[8,2,384,128]{3,2,1,0:T(8,128)(2,1)} %constant.6.clone.hi_hbm.hi_ref, bf16[8,2,384,128]{3,2,1,0:T(8,128)(2,1)} %constant.7.clone.lo_hbm.lo_ref), custom_call_target="tpu_custom_call" | custom-call | tf_op jit(solution)/shard_map/first/pallas_call | solution.py:486
  5.9 0.0 copy-start
  5.9 32.2 %all_to_all.10 = f32[2304,1,128]{2,1,0:T(1,128)S(1)} all-to-all(f32[2304,1,128]{2,1,0:T(1,128)} %bitcast.8), channel_id=1, replica_groups=mesh['modes'=4,'rows'=32] {'rows','modes'}, dimensions={0} | all-to-all | bytes 2359296 | tf_op jit(solution)/shard_map/all_to_all | solution.py:461
  38.0 0.0 copy-done.1
  38.0 0.0 copy-done
  38.0 9.9 %second.1 = f32[8,16,32,128]{3,2,1,0:T(8,128)} custom-call(f32[2304,128]{1,0:T(8,128)S(1)} %bitcast.6, bf16[8,2,384,128]{3,2,1,0:T(8,128)(2,1)S(1)} %copy-done, bf16[8,2,384,128]{3,2,1,0:T(8,128)(2,1)S(1)} %copy-done.1), custom_call_target="tpu_custom_call" | custom-call | tf_op jit(solution)/shard_map/second/pallas_call | solution.py:511
  47.9 0.0 copy-start.2
  47.9 5.0 %all-to-all-start.1 = ((f32[128,32,128]{2,1,0:T(8,128)}), f32[128,32,128]{2,1,0:T(8,128)}, u32[]{:S(2)}, u32[]{:S(2)}) async-start(f32[128,32,128]{2,1,0:T(8,128)} %bitcast.7), calls=%async_computation.1 | async-start | bytes 4194304 | tf_op jit(solution)/shard_map/all_to_all | solution.py:461
  53.0 0.0 copy-done.2
  53.0 2.0 %collective-permute-start.2 = (f32[1,2]{1,0:T(1,128)S(1)}, f32[1,2]{1,0:T(1,128)S(1)}, u32[]{:S(2)}, u32[]{:S(2)}) collective-permute-start(f32[1,2]{1,0:T(1,128)S(1)} %bitcast.9), channel_id=1, source_target_pairs={{0,96},{32,64},{64,32},{96,0},{1,97},{33,65},{65,33},{97,1},{2,98}... | collective-permute-start | bytes 32 | tf_op jit(solution)/shard_map/ppermute | solution.py:465
  55.0 0.7 collective-permute-start.1
  55.7 0.0 collective-permute-start
  55.7 2.0 %collective-permute-done.2 = f32[1,2]{1,0:T(1,128)S(1)} collective-permute-done((f32[1,2]{1,0:T(1,128)S(1)}, f32[1,2]{1,0:T(1,128)S(1)}, u32[]{:S(2)}, u32[]{:S(2)}) %collective-permute-start.2) | collective-permute-done | bytes 40 | tf_op jit(solution)/shard_map/ppermute | solution.py:465
  57.7 0.1 collective-permute-done.1
  57.8 0.0 collective-permute-done
  57.8 0.1 broadcast_in_dim.7
  57.9 24.7 %all-to-all-done.1.in_hbm = f32[128,32,128]{2,1,0:T(8,128)} async-done(((f32[128,32,128]{2,1,0:T(8,128)}), f32[128,32,128]{2,1,0:T(8,128)}, u32[]{:S(2)}, u32[]{:S(2)}) %all-to-all-start.1) | async-done | bytes 2097184 | tf_op jit(solution)/shard_map/all_to_all | solution.py:461
  82.6 0.1 broadcast_in_dim.8.weight_ref
  82.6 6.9 %third.1 = (f32[16,512]{1,0:T(8,128)S(1)}, f32[16,512]{1,0:T(8,128)S(1)}, f32[16,512]{1,0:T(8,128)S(1)}, f32[16,512]{1,0:T(8,128)S(1)}) custom-call(f32[128,32,128]{2,1,0:T(8,128)} %all-to-all-done.1.in_hbm, f32[8,1,128]{2,1,0:T(1,128)S(1)} %broadcast_in_dim.8.weight_ref, bf16[8,2,384,128]{3,2,1,0:T(8,128)(2,1)S(1)} %copy-done, ...), custom_call_target="tpu_custom_call" | custom-call | tf_op jit(solution)/shard_map/third/pallas_call | solution.py:529
  89.6 1.3 %collective-permute-start.3 = (f32[16,512]{1,0:T(8,128)S(1)}, f32[16,512]{1,0:T(8,128)S(1)}, u32[]{:S(2)}, u32[]{:S(2)}) collective-permute-start(f32[16,512]{1,0:T(8,128)S(1)} %get-tuple-element.10), channel_id=1, source_target_pairs={{0,32},{32,0},{64,96},{96,64},{1,33},{33,1},{65,97},{97,65},{2,34}... | collective-permute-start | bytes 98312 | tf_op jit(solution)/shard_map/ppermute | solution.py:465
  90.9 0.5 collective-permute-start.4
  91.4 1.2 %collective-permute-start.5 = (f32[16,512]{1,0:T(8,128)S(1)}, f32[16,512]{1,0:T(8,128)S(1)}, u32[]{:S(2)}, u32[]{:S(2)}) collective-permute-start(f32[16,512]{1,0:T(8,128)S(1)} %get-tuple-element.12), channel_id=1, source_target_pairs={{0,96},{32,64},{64,32},{96,0},{1,97},{33,65},{65,33},{97,1},{2,98}... | collective-permute-start | bytes 98312 | tf_op jit(solution)/shard_map/ppermute | solution.py:465
  92.6 0.0 collective-permute-done.3.in1
  92.6 1.0 %collective-permute-done.4.in2 = f32[16,512]{1,0:T(8,128)S(1)} collective-permute-done((f32[16,512]{1,0:T(8,128)S(1)}, f32[16,512]{1,0:T(8,128)S(1)}, u32[]{:S(2)}, u32[]{:S(2)}) %collective-permute-start.4) | collective-permute-done | bytes 32800 | tf_op jit(solution)/shard_map/ppermute | solution.py:465
  93.7 1.3 %collective-permute-done.5.in3 = f32[16,512]{1,0:T(8,128)S(1)} collective-permute-done((f32[16,512]{1,0:T(8,128)S(1)}, f32[16,512]{1,0:T(8,128)S(1)}, u32[]{:S(2)}, u32[]{:S(2)}) %collective-permute-start.5) | collective-permute-done | bytes 32800 | tf_op jit(solution)/shard_map/ppermute | solution.py:465
  95.0 0.7 last.1
  (1 shorter events, 0.0 us)
Async XLA Ops:
  0.0 38.0 %copy-start.1 = (bf16[8,2,384,128]{3,2,1,0:T(8,128)(2,1)S(1)}, bf16[8,2,384,128]{3,2,1,0:T(8,128)(2,1)}, u32[]{:S(2)}) copy-start(bf16[8,2,384,128]{3,2,1,0:T(8,128)(2,1)} %constant.7.clone.lo_hbm.lo_ref) | copy-start | bytes 4718596
  5.9 32.2 %copy-start = (bf16[8,2,384,128]{3,2,1,0:T(8,128)(2,1)S(1)}, bf16[8,2,384,128]{3,2,1,0:T(8,128)(2,1)}, u32[]{:S(2)}) copy-start(bf16[8,2,384,128]{3,2,1,0:T(8,128)(2,1)} %constant.6.clone.hi_hbm.hi_ref) | copy-start | bytes 4718596
  47.9 5.1 %copy-start.2 = (f32[2]{0:T(128)S(1)}, f32[2]{0:T(128)}, u32[]{:S(2)}) copy-start(f32[2]{0:T(128)} %param.6) | copy-start | bytes 28
  47.9 34.6 %all-to-all-start.1 = ((f32[128,32,128]{2,1,0:T(8,128)}), f32[128,32,128]{2,1,0:T(8,128)}, u32[]{:S(2)}, u32[]{:S(2)}) async-start(f32[128,32,128]{2,1,0:T(8,128)} %bitcast.7), calls=%async_computation.1 | async-start | bytes 4194304 | tf_op jit(solution)/shard_map/all_to_all | solution.py:461
  53.0 4.7 %collective-permute-start.2 = (f32[1,2]{1,0:T(1,128)S(1)}, f32[1,2]{1,0:T(1,128)S(1)}, u32[]{:S(2)}, u32[]{:S(2)}) collective-permute-start(f32[1,2]{1,0:T(1,128)S(1)} %bitcast.9), channel_id=1, source_target_pairs={{0,96},{32,64},{64,32},{96,0},{1,97},{33,65},{65,33},{97,1},{2,98}... | collective-permute-start | bytes 32 | tf_op jit(solution)/shard_map/ppermute | solution.py:465
  55.0 2.8 %collective-permute-start.1 = (f32[1,2]{1,0:T(1,128)S(1)}, f32[1,2]{1,0:T(1,128)S(1)}, u32[]{:S(2)}, u32[]{:S(2)}) collective-permute-start(f32[1,2]{1,0:T(1,128)S(1)} %bitcast.10), channel_id=1, source_target_pairs={{0,64},{32,96},{64,0},{96,32},{1,65},{33,97},{65,1},{97,33},{2,66}... | collective-permute-start | bytes 32 | tf_op jit(solution)/shard_map/ppermute | solution.py:465
  55.7 2.1 %collective-permute-start = (f32[1,2]{1,0:T(1,128)S(1)}, f32[1,2]{1,0:T(1,128)S(1)}, u32[]{:S(2)}, u32[]{:S(2)}) collective-permute-start(f32[1,2]{1,0:T(1,128)S(1)} %bitcast.11), channel_id=1, source_target_pairs={{0,32},{32,0},{64,96},{96,64},{1,33},{33,1},{65,97},{97,65},{2,34}... | collective-permute-start | bytes 32 | tf_op jit(solution)/shard_map/ppermute | solution.py:465
  89.6 3.0 %collective-permute-start.3 = (f32[16,512]{1,0:T(8,128)S(1)}, f32[16,512]{1,0:T(8,128)S(1)}, u32[]{:S(2)}, u32[]{:S(2)}) collective-permute-start(f32[16,512]{1,0:T(8,128)S(1)} %get-tuple-element.10), channel_id=1, source_target_pairs={{0,32},{32,0},{64,96},{96,64},{1,33},{33,1},{65,97},{97,65},{2,34}... | collective-permute-start | bytes 98312 | tf_op jit(solution)/shard_map/ppermute | solution.py:465
  90.9 2.8 %collective-permute-start.4 = (f32[16,512]{1,0:T(8,128)S(1)}, f32[16,512]{1,0:T(8,128)S(1)}, u32[]{:S(2)}, u32[]{:S(2)}) collective-permute-start(f32[16,512]{1,0:T(8,128)S(1)} %get-tuple-element.11), channel_id=1, source_target_pairs={{0,64},{32,96},{64,0},{96,32},{1,65},{33,97},{65,1},{97,33},{2,66}... | collective-permute-start | bytes 98312 | tf_op jit(solution)/shard_map/ppermute | solution.py:465
  91.4 3.6 %collective-permute-start.5 = (f32[16,512]{1,0:T(8,128)S(1)}, f32[16,512]{1,0:T(8,128)S(1)}, u32[]{:S(2)}, u32[]{:S(2)}) collective-permute-start(f32[16,512]{1,0:T(8,128)S(1)} %get-tuple-element.12), channel_id=1, source_target_pairs={{0,96},{32,64},{64,32},{96,0},{1,97},{33,65},{65,33},{97,1},{2,98}... | collective-permute-start | bytes 98312 | tf_op jit(solution)/shard_map/ppermute | solution.py:465
